TPU v7x, 256 devices: a whole 4x4x8 slice. The times are simulated.
256 devices in a mesh: dom: 32 (over x, z_hi, y), mode: 8 (over z_lo, core).
Axes of the slice: x: 4, y: 4, z: 8 (z_hi: 2, z_lo: 4; z = z_hi * 4 + z_lo), core: 2. Of those that a mesh axis runs over, the one named last changes fastest.
Arguments:
- iterate: float32 [256, 1024, 256], P('mode', 'dom'), may hold values from -6 to 6
- source: float32 [256, 1024, 256], P('mode', 'dom'), may hold values from -6 to 6
- mean_coef: float32 [1024, 256], P('dom'), may hold values from 0.5 to 2
- kl_fields: float32 [20, 1024, 256], P(None, 'dom'), may hold values from -1 to 1
- tri_index: int32 [5376, 3], replicated, may hold values from 0 to 255, as said below
- tri_value: float32 [5376], replicated, may hold values from 0.25 to 1.75, as said below
Outputs:
- updated: float32 [256, 1024, 256], P('mode', 'dom')
- residual: float32 [256, 1024, 256], P('mode', 'dom')
Inputs may be any that keep to these rules, and one draw needn't show every extreme that they name: `tri_index`: every pair of a mode i and a field l appears in exactly one entry; entries of field 0 have j = i; for fields 1 to 20 the entry (i, j, l) is listed together with (j, i, l), j differing from i; rows stand in a random order. `tri_value`: the entries (i, j, l) and (j, i, l) carry the same value.
All inputs are finite; a program needn't handle non-finite values.
Results may differ from a plain program's by a relative error of at most 0.0062.
Values may be sent and summed in bfloat16 or wider, within the bound.
A program may use at most 64 MiB of HBM per device.

v0:
```python
import jax
import jax.numpy as jnp
from jax import lax
from jax.sharding import PartitionSpec as P

P_SIZE = 256
L = 20
NZ = 16


cheb_center = 1.125
cheb_radius = 0.875


def padded_2(block, sides, width):
    for axis, dim in sides:
        count = lax.axis_size(axis)
        forward = [(i, i + 1) for i in range(count - 1)]
        backward = [(target, source) for source, target in forward]
        low = lax.ppermute(
            lax.slice_in_dim(block, block.shape[dim] - width, None, axis=dim), axis, forward
        )
        high = lax.ppermute(lax.slice_in_dim(block, 0, width, axis=dim), axis, backward)
        block = jnp.concatenate([low, block, high], axis=dim)
    return block


def shifted(field, offset):
    if offset > 0:
        filler = jnp.zeros(field.shape[:-1] + (offset,), field.dtype)
        return jnp.concatenate([field[..., offset:], filler], -1)
    amount = -offset
    filler = jnp.zeros(field.shape[:-1] + (amount,), field.dtype)
    return jnp.concatenate([filler, field[..., :-amount]], -1)


def z_masks(cells, z_depth):
    z_place = jnp.arange(cells) % z_depth
    return ((z_place < z_depth - 1).astype(jnp.float32), (z_place > 0).astype(jnp.float32))


def face_weights(padded_coef, upper_mask, lower_mask, z_depth):
    centre = padded_coef[:, 1:-1]
    return (
        0.5 * (centre + padded_coef[:, 2:]),
        0.5 * (centre + padded_coef[:, :-2]),
        0.5 * (centre + shifted(centre, z_depth)),
        0.5 * (centre + shifted(centre, -z_depth)),
        0.5 * (centre + shifted(centre, 1) * upper_mask),
        0.5 * (centre + shifted(centre, -1) * lower_mask),
    )


def apply_stencil(padded, face_set, upper_mask, lower_mask, z_depth):
    centre = padded[:, 1:-1]
    result = face_set[0] * (centre - padded[:, 2:]) + face_set[1] * (centre - padded[:, :-2])
    result = (
        result
        + face_set[2] * (centre - shifted(centre, z_depth))
        + face_set[3] * (centre - shifted(centre, -z_depth))
    )
    result = result + face_set[4] * (centre - shifted(centre, 1) * upper_mask)
    return result + face_set[5] * (centre - shifted(centre, -1) * lower_mask)


def mix_apply(matrices, flat, weights, modes_out, rows_out, cells, upper_mask, lower_mask):

    def accumulate(field_index, total):
        matrix = lax.dynamic_index_in_dim(matrices, field_index, 1, keepdims=False)
        mixed = jnp.dot(matrix, flat, preferred_element_type=jnp.float32).reshape(
            modes_out, rows_out + 2, cells
        )
        faces_here = tuple(
            (lax.dynamic_index_in_dim(weight, field_index, 0, keepdims=False) for weight in weights)
        )
        return total + apply_stencil(mixed, faces_here, upper_mask, lower_mask, NZ)

    return lax.fori_loop(0, L + 1, accumulate, jnp.zeros((modes_out, rows_out, cells), jnp.float32))


def body(iterate, source, mean_coef, kl_fields, tri_index, tri_value):
    modes_here, rows_here, cells = iterate.shape
    coef = jnp.concatenate([mean_coef[None], kl_fields], 0)
    padded_coef = padded_2(coef, (("dom", 1),), 1)
    upper_mask, lower_mask = z_masks(cells, NZ)
    face_set = face_weights(padded_coef, upper_mask, lower_mask, NZ)
    dense = jnp.zeros((P_SIZE, L + 1, P_SIZE), jnp.float32)
    dense = dense.at[tri_index[:, 0], tri_index[:, 2], tri_index[:, 1]].add(tri_value)
    rounded = iterate.astype(jnp.bfloat16)
    own_rows = lax.dynamic_slice_in_dim(
        dense, lax.axis_index("mode") * modes_here, modes_here, 0
    ).astype(jnp.bfloat16)
    gathered = lax.all_gather(rounded, "mode", axis=0, tiled=True)
    panels = padded_2(gathered, (("dom", 1),), 1)
    image = mix_apply(
        own_rows,
        panels.reshape(P_SIZE, -1),
        face_set,
        modes_here,
        rows_here,
        cells,
        upper_mask,
        lower_mask,
    )
    residual = source - image
    mean_faces = tuple((weight[0] for weight in face_set))
    diag = (
        mean_faces[0]
        + mean_faces[1]
        + mean_faces[2]
        + mean_faces[3]
        + mean_faces[4]
        + mean_faces[5]
    )
    sigma = cheb_center / cheb_radius
    rho_zero = 1.0 / sigma
    rho_one = 1.0 / (2.0 * sigma - rho_zero)
    first = residual / (cheb_center * diag)
    padded_first = padded_2(first, (("dom", 1),), 1)
    smoothed = residual - apply_stencil(padded_first, mean_faces, upper_mask, lower_mask, NZ)
    second = rho_one * rho_zero * first + 2.0 * rho_one / cheb_radius * smoothed / diag
    return (iterate + first + second, residual)


def solution(mesh):
    return jax.shard_map(
        body,
        mesh=mesh,
        in_specs=(
            P("mode", "dom", None),
            P("mode", "dom", None),
            P("dom", None),
            P(None, "dom", None),
            P(),
            P(),
        ),
        out_specs=(P("mode", "dom", None), P("mode", "dom", None)),
        check_vma=False,
    )
```

profile of v0, /device:TPU:6, one launch (start us, length us, event | category | flops | bytes accessed | tf_op | source)
XLA Modules:
  0.0 377.2 jit_solution(9868509851415721504)
XLA Ops:
  7.2 2.1 convert_element_type.29
  10.4 11.8 %collective-permute-start = (f32[21,1,256]{2,1,0:T(1,128)S(1)}, f32[21,1,256]{2,1,0:T(1,128)S(1)}, u32[]{:S(2)}, u32[]{:S(2)}) collective-permute-start(f32[21,1,256]{2,1,0:T(1,128)S(1)} %get-tuple-element.304), channel_id=1, source_target_pairs={{8,0},{16,8},{24,16},{32,24},{40,32},{48,40},{56,48},{64,56},{72,6... | collective-permute-start | bytes 64520 | tf_op jit(solution)/shard_map/ppermute | solution.py:23
  22.2 1.9 collective-permute-start.3
  26.9 31.5 %scatter_custom_fusion = f32[1376256]{0:T(1024)} fusion(s32[5376]{0:T(1024)S(1)} %broadcast_select_fusion, f32[5376]{0:T(1024)} %param.13, f32[]{:T(128)} %constant.83.clone.1), kind=kCustom, calls=%fused_computation.27 | custom fusion | flops 5376 | bytes 5505536
  58.4 4.4 %reshape.33 = bf16[21,256,256]{2,1,0:T(8,128)(2,1)S(1)} reshape(f32[1376256]{0:T(1024)} %scatter_custom_fusion) | data formatting | bytes 8257536
  65.1 2.3 fusion.39
  67.8 2.0 fusion.45
  69.8 3.4 collective-permute-start.1
  73.2 9.4 %collective-permute-start.2 = (bf16[256,1,256]{2,0,1:T(8,128)(2,1)S(1)}, bf16[256,1,256]{2,0,1:T(8,128)(2,1)S(1)}, u32[]{:S(2)}, u32[]{:S(2)}) collective-permute-start(bf16[256,1,256]{2,0,1:T(8,128)(2,1)S(1)} %copy.17), channel_id=1, source_target_pairs={{8,0},{16,8},{24,16},{32,24},{40,32},{48,40},{56,48},{64,56},{72,6... | collective-permute-start | bytes 393224 | tf_op jit(solution)/shard_map/ppermute | solution.py:23
  84.1 7.6 %copy.19 = bf16[256,32,256]{0,2,1:T(8,128)(2,1)} copy(bf16[256,32,256]{2,1,0:T(8,128)(2,1)} %all-gather.2.cloned.1.call-done) | data formatting | bytes 8388608 | tf_op jit(solution)/shard_map/all_gather | solution.py:93
  91.9 4.0 %pad_maximum_fusion = bf16[256,34,256]{0,2,1:T(8,128)(2,1)} fusion(bf16[256,1,256]{0,2,1:T(8,128)(2,1)S(1)} %copy.20, bf16[256,32,256]{0,2,1:T(8,128)(2,1)} %copy.19, bf16[256,1,256]{0,2,1:T(8,128)(2,1)S(1)} %copy.18), kind=kLoop, calls=%fused_computation.26 | loop fusion | flops 4456448 | bytes 8912896 | tf_op jit(solution)/shard_map/concatenate | solution.py:24
  95.9 249.9 %while.14 = (s32[]{:T(128)}, f32[32,32,256]{2,0,1:T(8,128)}, f32[21,32,256]{2,1,0:T(8,128)}, bf16[32,21,256]{2,0,1:T(8,128)(2,1)}, bf16[256,8704]{0,1:T(8,128)(2...) while((s32[]{:T(128)}, f32[32,32,256]{2,0,1:T(8,128)}, ...), condition=%wide.region_2.3_spmd.clone, body=%wide.region_1.2_spmd.clone.sunk | while | flops 148113920 | bytes 23589516 | solution.py:78
  95.9 3.7 fusion.58
  104.0 3.5 fusion.61
  107.5 3.7 fusion.58
  115.6 3.8 %fusion.61 = f32[32,32,256]{2,0,1:T(8,128)} fusion(f32[32,34,256]{2,0,1:T(8,128)S(1)} %fusion.58, f32[32,32,256]{2,0,1:T(8,128)} %get-tuple-element.413, f32[32,32,255]{2,0,1:T(8,128)S(1)} %get-tuple-element.388, f32[32,32,255]{2,0,1:T(8,128)S(1)} %get-tuple-element.389, f32[32,32,240]{2,0,1:T(8,128)} %get-tuple-element.390, ...), kind=kLoop, calls=%fused_computation.10.clone.1 | loop fusion | flops 5505024 | bytes 9496577 | tf_op jit(solution)/shard_map/while/body/eval_jaxpr/add | solution.py:76
  119.4 3.7 fusion.58
  127.5 3.8 %fusion.61 = f32[32,32,256]{2,0,1:T(8,128)} fusion(f32[32,34,256]{2,0,1:T(8,128)S(1)} %fusion.58, f32[32,32,256]{2,0,1:T(8,128)} %get-tuple-element.413, f32[32,32,255]{2,0,1:T(8,128)S(1)} %get-tuple-element.388, f32[32,32,255]{2,0,1:T(8,128)S(1)} %get-tuple-element.389, f32[32,32,240]{2,0,1:T(8,128)} %get-tuple-element.390, ...), kind=kLoop, calls=%fused_computation.10.clone.1 | loop fusion | flops 5505024 | bytes 9496577 | tf_op jit(solution)/shard_map/while/body/eval_jaxpr/add | solution.py:76
  131.3 3.7 fusion.58
  139.4 3.8 %fusion.61 = f32[32,32,256]{2,0,1:T(8,128)} fusion(f32[32,34,256]{2,0,1:T(8,128)S(1)} %fusion.58, f32[32,32,256]{2,0,1:T(8,128)} %get-tuple-element.413, f32[32,32,255]{2,0,1:T(8,128)S(1)} %get-tuple-element.388, f32[32,32,255]{2,0,1:T(8,128)S(1)} %get-tuple-element.389, f32[32,32,240]{2,0,1:T(8,128)} %get-tuple-element.390, ...), kind=kLoop, calls=%fused_computation.10.clone.1 | loop fusion | flops 5505024 | bytes 9496577 | tf_op jit(solution)/shard_map/while/body/eval_jaxpr/add | solution.py:76
  143.2 3.7 fusion.58
  147.3 1.7 fusion.60
  151.3 3.8 %fusion.61 = f32[32,32,256]{2,0,1:T(8,128)} fusion(f32[32,34,256]{2,0,1:T(8,128)S(1)} %fusion.58, f32[32,32,256]{2,0,1:T(8,128)} %get-tuple-element.413, f32[32,32,255]{2,0,1:T(8,128)S(1)} %get-tuple-element.388, f32[32,32,255]{2,0,1:T(8,128)S(1)} %get-tuple-element.389, f32[32,32,240]{2,0,1:T(8,128)} %get-tuple-element.390, ...), kind=kLoop, calls=%fused_computation.10.clone.1 | loop fusion | flops 5505024 | bytes 9496577 | tf_op jit(solution)/shard_map/while/body/eval_jaxpr/add | solution.py:76
  155.1 3.7 fusion.58
  163.2 3.8 %fusion.61 = f32[32,32,256]{2,0,1:T(8,128)} fusion(f32[32,34,256]{2,0,1:T(8,128)S(1)} %fusion.58, f32[32,32,256]{2,0,1:T(8,128)} %get-tuple-element.413, f32[32,32,255]{2,0,1:T(8,128)S(1)} %get-tuple-element.388, f32[32,32,255]{2,0,1:T(8,128)S(1)} %get-tuple-element.389, f32[32,32,240]{2,0,1:T(8,128)} %get-tuple-element.390, ...), kind=kLoop, calls=%fused_computation.10.clone.1 | loop fusion | flops 5505024 | bytes 9496577 | tf_op jit(solution)/shard_map/while/body/eval_jaxpr/add | solution.py:76
  167.0 3.7 fusion.58
  171.1 1.7 fusion.60
  175.1 3.8 %fusion.61 = f32[32,32,256]{2,0,1:T(8,128)} fusion(f32[32,34,256]{2,0,1:T(8,128)S(1)} %fusion.58, f32[32,32,256]{2,0,1:T(8,128)} %get-tuple-element.413, f32[32,32,255]{2,0,1:T(8,128)S(1)} %get-tuple-element.388, f32[32,32,255]{2,0,1:T(8,128)S(1)} %get-tuple-element.389, f32[32,32,240]{2,0,1:T(8,128)} %get-tuple-element.390, ...), kind=kLoop, calls=%fused_computation.10.clone.1 | loop fusion | flops 5505024 | bytes 9496577 | tf_op jit(solution)/shard_map/while/body/eval_jaxpr/add | solution.py:76
  179.0 3.7 fusion.58
  187.1 3.8 %fusion.61 = f32[32,32,256]{2,0,1:T(8,128)} fusion(f32[32,34,256]{2,0,1:T(8,128)S(1)} %fusion.58, f32[32,32,256]{2,0,1:T(8,128)} %get-tuple-element.413, f32[32,32,255]{2,0,1:T(8,128)S(1)} %get-tuple-element.388, f32[32,32,255]{2,0,1:T(8,128)S(1)} %get-tuple-element.389, f32[32,32,240]{2,0,1:T(8,128)} %get-tuple-element.390, ...), kind=kLoop, calls=%fused_computation.10.clone.1 | loop fusion | flops 5505024 | bytes 9496577 | tf_op jit(solution)/shard_map/while/body/eval_jaxpr/add | solution.py:76
  190.9 3.7 fusion.58
  194.9 1.7 fusion.60
  199.0 3.8 %fusion.61 = f32[32,32,256]{2,0,1:T(8,128)} fusion(f32[32,34,256]{2,0,1:T(8,128)S(1)} %fusion.58, f32[32,32,256]{2,0,1:T(8,128)} %get-tuple-element.413, f32[32,32,255]{2,0,1:T(8,128)S(1)} %get-tuple-element.388, f32[32,32,255]{2,0,1:T(8,128)S(1)} %get-tuple-element.389, f32[32,32,240]{2,0,1:T(8,128)} %get-tuple-element.390, ...), kind=kLoop, calls=%fused_computation.10.clone.1 | loop fusion | flops 5505024 | bytes 9496577 | tf_op jit(solution)/shard_map/while/body/eval_jaxpr/add | solution.py:76
  202.8 3.7 fusion.58
  210.9 3.8 %fusion.61 = f32[32,32,256]{2,0,1:T(8,128)} fusion(f32[32,34,256]{2,0,1:T(8,128)S(1)} %fusion.58, f32[32,32,256]{2,0,1:T(8,128)} %get-tuple-element.413, f32[32,32,255]{2,0,1:T(8,128)S(1)} %get-tuple-element.388, f32[32,32,255]{2,0,1:T(8,128)S(1)} %get-tuple-element.389, f32[32,32,240]{2,0,1:T(8,128)} %get-tuple-element.390, ...), kind=kLoop, calls=%fused_computation.10.clone.1 | loop fusion | flops 5505024 | bytes 9496577 | tf_op jit(solution)/shard_map/while/body/eval_jaxpr/add | solution.py:76
  214.7 3.7 fusion.58
  218.8 1.7 fusion.60
  222.8 3.8 %fusion.61 = f32[32,32,256]{2,0,1:T(8,128)} fusion(f32[32,34,256]{2,0,1:T(8,128)S(1)} %fusion.58, f32[32,32,256]{2,0,1:T(8,128)} %get-tuple-element.413, f32[32,32,255]{2,0,1:T(8,128)S(1)} %get-tuple-element.388, f32[32,32,255]{2,0,1:T(8,128)S(1)} %get-tuple-element.389, f32[32,32,240]{2,0,1:T(8,128)} %get-tuple-element.390, ...), kind=kLoop, calls=%fused_computation.10.clone.1 | loop fusion | flops 5505024 | bytes 9496577 | tf_op jit(solution)/shard_map/while/body/eval_jaxpr/add | solution.py:76
  226.6 3.7 fusion.58
  234.7 3.8 %fusion.61 = f32[32,32,256]{2,0,1:T(8,128)} fusion(f32[32,34,256]{2,0,1:T(8,128)S(1)} %fusion.58, f32[32,32,256]{2,0,1:T(8,128)} %get-tuple-element.413, f32[32,32,255]{2,0,1:T(8,128)S(1)} %get-tuple-element.388, f32[32,32,255]{2,0,1:T(8,128)S(1)} %get-tuple-element.389, f32[32,32,240]{2,0,1:T(8,128)} %get-tuple-element.390, ...), kind=kLoop, calls=%fused_computation.10.clone.1 | loop fusion | flops 5505024 | bytes 9496577 | tf_op jit(solution)/shard_map/while/body/eval_jaxpr/add | solution.py:76
  238.5 3.7 fusion.58
  242.6 1.7 fusion.60
  246.6 3.8 %fusion.61 = f32[32,32,256]{2,0,1:T(8,128)} fusion(f32[32,34,256]{2,0,1:T(8,128)S(1)} %fusion.58, f32[32,32,256]{2,0,1:T(8,128)} %get-tuple-element.413, f32[32,32,255]{2,0,1:T(8,128)S(1)} %get-tuple-element.388, f32[32,32,255]{2,0,1:T(8,128)S(1)} %get-tuple-element.389, f32[32,32,240]{2,0,1:T(8,128)} %get-tuple-element.390, ...), kind=kLoop, calls=%fused_computation.10.clone.1 | loop fusion | flops 5505024 | bytes 9496577 | tf_op jit(solution)/shard_map/while/body/eval_jaxpr/add | solution.py:76
  250.4 3.7 fusion.58
  258.5 3.8 %fusion.61 = f32[32,32,256]{2,0,1:T(8,128)} fusion(f32[32,34,256]{2,0,1:T(8,128)S(1)} %fusion.58, f32[32,32,256]{2,0,1:T(8,128)} %get-tuple-element.413, f32[32,32,255]{2,0,1:T(8,128)S(1)} %get-tuple-element.388, f32[32,32,255]{2,0,1:T(8,128)S(1)} %get-tuple-element.389, f32[32,32,240]{2,0,1:T(8,128)} %get-tuple-element.390, ...), kind=kLoop, calls=%fused_computation.10.clone.1 | loop fusion | flops 5505024 | bytes 9496577 | tf_op jit(solution)/shard_map/while/body/eval_jaxpr/add | solution.py:76
  262.4 3.7 fusion.58
  270.5 3.8 %fusion.61 = f32[32,32,256]{2,0,1:T(8,128)} fusion(f32[32,34,256]{2,0,1:T(8,128)S(1)} %fusion.58, f32[32,32,256]{2,0,1:T(8,128)} %get-tuple-element.413, f32[32,32,255]{2,0,1:T(8,128)S(1)} %get-tuple-element.388, f32[32,32,255]{2,0,1:T(8,128)S(1)} %get-tuple-element.389, f32[32,32,240]{2,0,1:T(8,128)} %get-tuple-element.390, ...), kind=kLoop, calls=%fused_computation.10.clone.1 | loop fusion | flops 5505024 | bytes 9496577 | tf_op jit(solution)/shard_map/while/body/eval_jaxpr/add | solution.py:76
  274.3 3.7 fusion.58
  282.4 3.8 %fusion.61 = f32[32,32,256]{2,0,1:T(8,128)} fusion(f32[32,34,256]{2,0,1:T(8,128)S(1)} %fusion.58, f32[32,32,256]{2,0,1:T(8,128)} %get-tuple-element.413, f32[32,32,255]{2,0,1:T(8,128)S(1)} %get-tuple-element.388, f32[32,32,255]{2,0,1:T(8,128)S(1)} %get-tuple-element.389, f32[32,32,240]{2,0,1:T(8,128)} %get-tuple-element.390, ...), kind=kLoop, calls=%fused_computation.10.clone.1 | loop fusion | flops 5505024 | bytes 9496577 | tf_op jit(solution)/shard_map/while/body/eval_jaxpr/add | solution.py:76
  286.2 3.7 fusion.58
  294.3 3.8 %fusion.61 = f32[32,32,256]{2,0,1:T(8,128)} fusion(f32[32,34,256]{2,0,1:T(8,128)S(1)} %fusion.58, f32[32,32,256]{2,0,1:T(8,128)} %get-tuple-element.413, f32[32,32,255]{2,0,1:T(8,128)S(1)} %get-tuple-element.388, f32[32,32,255]{2,0,1:T(8,128)S(1)} %get-tuple-element.389, f32[32,32,240]{2,0,1:T(8,128)} %get-tuple-element.390, ...), kind=kLoop, calls=%fused_computation.10.clone.1 | loop fusion | flops 5505024 | bytes 9496577 | tf_op jit(solution)/shard_map/while/body/eval_jaxpr/add | solution.py:76
  298.1 3.7 fusion.58
  306.2 3.8 %fusion.61 = f32[32,32,256]{2,0,1:T(8,128)} fusion(f32[32,34,256]{2,0,1:T(8,128)S(1)} %fusion.58, f32[32,32,256]{2,0,1:T(8,128)} %get-tuple-element.413, f32[32,32,255]{2,0,1:T(8,128)S(1)} %get-tuple-element.388, f32[32,32,255]{2,0,1:T(8,128)S(1)} %get-tuple-element.389, f32[32,32,240]{2,0,1:T(8,128)} %get-tuple-element.390, ...), kind=kLoop, calls=%fused_computation.10.clone.1 | loop fusion | flops 5505024 | bytes 9496577 | tf_op jit(solution)/shard_map/while/body/eval_jaxpr/add | solution.py:76
  310.0 3.7 fusion.58
  318.1 3.8 %fusion.61 = f32[32,32,256]{2,0,1:T(8,128)} fusion(f32[32,34,256]{2,0,1:T(8,128)S(1)} %fusion.58, f32[32,32,256]{2,0,1:T(8,128)} %get-tuple-element.413, f32[32,32,255]{2,0,1:T(8,128)S(1)} %get-tuple-element.388, f32[32,32,255]{2,0,1:T(8,128)S(1)} %get-tuple-element.389, f32[32,32,240]{2,0,1:T(8,128)} %get-tuple-element.390, ...), kind=kLoop, calls=%fused_computation.10.clone.1 | loop fusion | flops 5505024 | bytes 9496577 | tf_op jit(solution)/shard_map/while/body/eval_jaxpr/add | solution.py:76
  321.9 3.7 fusion.58
  330.0 3.8 %fusion.61 = f32[32,32,256]{2,0,1:T(8,128)} fusion(f32[32,34,256]{2,0,1:T(8,128)S(1)} %fusion.58, f32[32,32,256]{2,0,1:T(8,128)} %get-tuple-element.413, f32[32,32,255]{2,0,1:T(8,128)S(1)} %get-tuple-element.388, f32[32,32,255]{2,0,1:T(8,128)S(1)} %get-tuple-element.389, f32[32,32,240]{2,0,1:T(8,128)} %get-tuple-element.390, ...), kind=kLoop, calls=%fused_computation.10.clone.1 | loop fusion | flops 5505024 | bytes 9496577 | tf_op jit(solution)/shard_map/while/body/eval_jaxpr/add | solution.py:76
  333.9 3.7 fusion.58
  342.0 3.8 %fusion.61 = f32[32,32,256]{2,0,1:T(8,128)} fusion(f32[32,34,256]{2,0,1:T(8,128)S(1)} %fusion.58, f32[32,32,256]{2,0,1:T(8,128)} %get-tuple-element.413, f32[32,32,255]{2,0,1:T(8,128)S(1)} %get-tuple-element.388, f32[32,32,255]{2,0,1:T(8,128)S(1)} %get-tuple-element.389, f32[32,32,240]{2,0,1:T(8,128)} %get-tuple-element.390, ...), kind=kLoop, calls=%fused_computation.10.clone.1 | loop fusion | flops 5505024 | bytes 9496577 | tf_op jit(solution)/shard_map/while/body/eval_jaxpr/add | solution.py:76
  345.8 2.2 broadcast_divide_fusion
  348.5 6.8 %collective-permute-start.4 = (f32[32,1,256]{2,1,0:T(1,128)S(1)}, f32[32,1,256]{2,1,0:T(1,128)S(1)}, u32[]{:S(2)}, u32[]{:S(2)}) collective-permute-start(f32[32,1,256]{2,1,0:T(1,128)S(1)} %get-tuple-element.291), channel_id=1, source_target_pairs={{8,0},{16,8},{24,16},{32,24},{40,32},{48,40},{56,48},{64,56},{72,6... | collective-permute-start | bytes 98312 | tf_op jit(solution)/shard_map/ppermute | solution.py:23
  355.3 1.9 collective-permute-start.5
  357.6 10.4 %collective-permute-done.5 = f32[32,1,256]{2,1,0:T(1,128)S(1)} collective-permute-done((f32[32,1,256]{2,1,0:T(1,128)S(1)}, f32[32,1,256]{2,1,0:T(1,128)S(1)}, u32[]{:S(2)}, u32[]{:S(2)}) %collective-permute-start.5) | collective-permute-done | bytes 32800 | tf_op jit(solution)/shard_map/ppermute | solution.py:20
  368.0 2.3 fusion.29
  (162 shorter events, 93.5 us)
Async XLA Ops:
  7.2 60.6 %all-gather.2.cloned.1.call-start = ((), (), s32[]{:S(2)}) async-start(), calls=%async_computation | async-start | bytes 4718592 | tf_op jit(solution)/shard_map/all_gather | solution.py:93
  10.4 54.7 %collective-permute-start = (f32[21,1,256]{2,1,0:T(1,128)S(1)}, f32[21,1,256]{2,1,0:T(1,128)S(1)}, u32[]{:S(2)}, u32[]{:S(2)}) collective-permute-start(f32[21,1,256]{2,1,0:T(1,128)S(1)} %get-tuple-element.304), channel_id=1, source_target_pairs={{8,0},{16,8},{24,16},{32,24},{40,32},{48,40},{56,48},{64,56},{72,6... | collective-permute-start | bytes 64520 | tf_op jit(solution)/shard_map/ppermute | solution.py:23
  22.2 41.9 %collective-permute-start.3 = (f32[21,1,256]{2,1,0:T(1,128)S(1)}, f32[21,1,256]{2,1,0:T(1,128)S(1)}, u32[]{:S(2)}, u32[]{:S(2)}) collective-permute-start(f32[21,1,256]{2,1,0:T(1,128)S(1)} %get-tuple-element.305), channel_id=1, source_target_pairs={{0,8},{8,16},{16,24},{24,32},{32,40},{40,48},{48,56},{56,64},{64,7... | collective-permute-start | bytes 64520 | tf_op jit(solution)/shard_map/ppermute | solution.py:20
  58.4 5.2 %copy-start = (f32[20,32,256]{2,1,0:T(8,128)S(1)}, f32[20,32,256]{2,1,0:T(8,128)}, u32[]{:S(2)}) copy-start(f32[20,32,256]{2,1,0:T(8,128)} %param.11) | copy-start | bytes 1966084
  58.4 5.2 %copy-start.3 = (f32[32,256]{1,0:T(8,128)S(1)}, f32[32,256]{1,0:T(8,128)}, u32[]{:S(2)}) copy-start(f32[32,256]{1,0:T(8,128)} %param.10) | copy-start | bytes 98308
  69.8 21.9 %collective-permute-start.1 = (bf16[256,1,256]{2,0,1:T(8,128)(2,1)S(1)}, bf16[256,1,256]{2,0,1:T(8,128)(2,1)S(1)}, u32[]{:S(2)}, u32[]{:S(2)}) collective-permute-start(bf16[256,1,256]{2,0,1:T(8,128)(2,1)S(1)} %copy.16), channel_id=1, source_target_pairs={{0,8},{8,16},{16,24},{24,32},{32,40},{40,48},{48,56},{56,64},{64,7... | collective-permute-start | bytes 393224 | tf_op jit(solution)/shard_map/ppermute | solution.py:20
  73.2 18.6 %collective-permute-start.2 = (bf16[256,1,256]{2,0,1:T(8,128)(2,1)S(1)}, bf16[256,1,256]{2,0,1:T(8,128)(2,1)S(1)}, u32[]{:S(2)}, u32[]{:S(2)}) collective-permute-start(bf16[256,1,256]{2,0,1:T(8,128)(2,1)S(1)} %copy.17), channel_id=1, source_target_pairs={{8,0},{16,8},{24,16},{32,24},{40,32},{48,40},{56,48},{64,56},{72,6... | collective-permute-start | bytes 393224 | tf_op jit(solution)/shard_map/ppermute | solution.py:23
  348.0 22.4 %copy-start.2 = (f32[32,32,256]{2,1,0:T(8,128)}, f32[32,32,256]{2,1,0:T(8,128)S(1)}, u32[]{:S(2)}) copy-start(f32[32,32,256]{2,1,0:T(8,128)S(1)} %get-tuple-element.270) | copy-start | bytes 3145732
  348.0 20.0 %copy-start.1 = (f32[32,32,256]{2,1,0:T(8,128)S(1)}, f32[32,32,256]{2,1,0:T(8,128)}, u32[]{:S(2)}) copy-start(f32[32,32,256]{2,1,0:T(8,128)} %param.8) | copy-start | bytes 3145732
  348.0 20.0 %copy-start.4 = (f32[32,256]{1,0:T(8,128)S(1)}, f32[32,256]{1,0:T(8,128)}, u32[]{:S(2)}) copy-start(f32[32,256]{1,0:T(8,128)} %get-tuple-element.296) | copy-start | bytes 98308
  348.0 20.0 %copy-start.5 = (f32[32,256]{1,0:T(8,128)S(1)}, f32[32,256]{1,0:T(8,128)}, u32[]{:S(2)}) copy-start(f32[32,256]{1,0:T(8,128)} %get-tuple-element.297) | copy-start | bytes 98308
  348.0 20.0 %copy-start.6 = (f32[32,256]{1,0:T(8,128)S(1)}, f32[32,256]{1,0:T(8,128)}, u32[]{:S(2)}) copy-start(f32[32,256]{1,0:T(8,128)} %get-tuple-element.298) | copy-start | bytes 98308
  348.5 9.1 %collective-permute-start.4 = (f32[32,1,256]{2,1,0:T(1,128)S(1)}, f32[32,1,256]{2,1,0:T(1,128)S(1)}, u32[]{:S(2)}, u32[]{:S(2)}) collective-permute-start(f32[32,1,256]{2,1,0:T(1,128)S(1)} %get-tuple-element.291), channel_id=1, source_target_pairs={{8,0},{16,8},{24,16},{32,24},{40,32},{48,40},{56,48},{64,56},{72,6... | collective-permute-start | bytes 98312 | tf_op jit(solution)/shard_map/ppermute | solution.py:23
  355.3 12.7 %collective-permute-start.5 = (f32[32,1,256]{2,1,0:T(1,128)S(1)}, f32[32,1,256]{2,1,0:T(1,128)S(1)}, u32[]{:S(2)}, u32[]{:S(2)}) collective-permute-start(f32[32,1,256]{2,1,0:T(1,128)S(1)} %get-tuple-element.292), channel_id=1, source_target_pairs={{0,8},{8,16},{16,24},{24,32},{32,40},{40,48},{48,56},{56,64},{64,7... | collective-permute-start | bytes 98312 | tf_op jit(solution)/shard_map/ppermute | solution.py:20
Sparse Core Ops, SparseCore 0:
  10.3 57.4 all-gather.1
where the time goes:
time: 383 us; the launch traced here: 377 us
  other arithmetic  131 us (34%)
  local copies, waits for them, and re-layouts  108 us (28%)
  matrix products  77 us (20%)
  starting transfers between devices  35.2 us (9%)
  between operations  14.3 us (4%)
  waiting for transfers between devices  10.9 us (3%)
    add x21, other arithmetic, accumulate(): return total + apply_stencil(mixed, faces_here, upper_mask, lower_mask, NZ)  79.8 us
    dot_general x21, matrix products, accumulate(): jnp.dot(matrix, flat, preferred_element_type=jnp.float32)  77 us
    slice x44, local copies, waits for them, and re-layouts, shifted(): return jnp.concatenate([field[..., offset:], filler], -1)  44.3 us
    unnamed x5, other arithmetic  33.1 us
    ppermute x3, starting transfers between devices, padded_2(): lax.ppermute(lax.slice_in_dim(block, 0, width, axis=dim), axis, backward)  28 us
    mul x21, local copies, waits for them, and re-layouts, apply_stencil(): return result + face_set[5] * (centre - shifted(centre, -1) * lower_mask)  16.4 us
    mul x21, local copies, waits for them, and re-layouts, apply_stencil(): face_set[3] * (centre - shifted(centre, -z_depth))  16.4 us
    mul x21, local copies, waits for them, and re-layouts, apply_stencil(): face_set[1] * (centre - padded[:, :-2])  16.4 us
  transfers between devices with their start and end apart: 7, of which 2 were waited for; matrix products, arithmetic and copies ran while one was open for 14% of the time, Pallas kernels for 0%

commit v1 on v0

v1 whole, which is shorter than its diff:
```python
import jax
import jax.numpy as jnp
from jax import lax
from jax.experimental import pallas as pl
from jax.experimental.pallas import tpu as pltpu
from jax.sharding import PartitionSpec as P

P_SIZE = 256
NF = 21
NZ = 16
CELLS = 256
IB = 32
NIB = P_SIZE // IB
ENTRIES = P_SIZE * NF

cheb_center = 1.125
cheb_radius = 0.875
sigma = cheb_center / cheb_radius
rho_zero = 1.0 / sigma
rho_one = 1.0 / (2.0 * sigma - rho_zero)

f32 = jnp.float32
bf16 = jnp.bfloat16
i32 = jnp.int32


def iota(shape, dim):
    return lax.broadcasted_iota(i32, shape, dim)


def plane_neighbours():
    q = iota((CELLS, CELLS), 0)
    p = iota((CELLS, CELLS), 1)
    far = jnp.abs(q - p)
    same = (q >> 4) == (p >> 4)
    return jnp.where((far == NZ) | ((far == 1) & same), 1.0, 0.0).astype(bf16)


def build_mixing(tri_ref, val_ref, mix_ref, table_ref):
    mode = iota((P_SIZE, 256), 0)
    level = iota((32, 256), 0)

    def gather(step, total):
        here = pl.ds(pl.multiple_of(step * 256, 256), 256)
        hot = jnp.where(mode == tri_ref[0:1, here], 1.0, 0.0).astype(bf16)
        mine = level == tri_ref[2:3, here]
        coef = jnp.where(mine, val_ref[0:1, here], 0.0).astype(bf16)
        trial = jnp.where(mine, tri_ref[1:2, here].astype(f32), 0.0).astype(bf16)
        both = jnp.concatenate([coef, trial], 0)
        return total + lax.dot_general(
            hot, both, (((1,), (1,)), ((), ())), preferred_element_type=f32
        )

    table_ref[...] = lax.fori_loop(0, ENTRIES // 256, gather, jnp.zeros((P_SIZE, 64), f32))
    column = iota((P_SIZE, P_SIZE), 1).astype(f32)
    for l in range(NF):
        coef = table_ref[:, l : l + 1]
        trial = table_ref[:, 32 + l : 33 + l]
        panel = jnp.where(column == trial, coef, 0.0).astype(bf16)
        mix_ref[:, l * IB : (l + 1) * IB, :] = panel.reshape(NIB, IB, P_SIZE)


def swap_matrix(major, minor):
    n = major * minor
    r = iota((n, n), 0)
    c = iota((n, n), 1)
    shift = minor.bit_length() - 1
    wanted = (r & (minor - 1)) * major + (r >> shift)
    return jnp.where(c == wanted, 1.0, 0.0).astype(bf16)


def prepare_kernel(tri_ref, val_ref, it_ref, mix_ref, rows_ref, table_ref):
    swap = swap_matrix(32, 16)
    for g in range(2):
        block = it_ref[16 * g : 16 * (g + 1)].astype(bf16).reshape(512, CELLS)
        turned = jnp.dot(swap, block, preferred_element_type=f32).astype(bf16)
        rows_ref[:, 16 * g : 16 * (g + 1), :] = turned.reshape(32, 16, CELLS)
    build_mixing(tri_ref, val_ref, mix_ref, table_ref)


def lane_neighbours(x, z_place, place):
    up = jnp.where(z_place < NZ - 1, pltpu.roll(x, CELLS - 1, x.ndim - 1), 0.0)
    down = jnp.where(z_place > 0, pltpu.roll(x, 1, x.ndim - 1), 0.0)
    far = jnp.where(place < CELLS - NZ, pltpu.roll(x, CELLS - NZ, x.ndim - 1), 0.0)
    near = jnp.where(place >= NZ, pltpu.roll(x, NZ, x.ndim - 1), 0.0)
    return up + down + far + near


def image_kernel(r_ref, mix_ref, b_ref, out_ref, g_ref, nb_ref, s_ref, t_ref):
    near = plane_neighbours()
    place = iota((24, CELLS), 1)
    for x in range(4):
        nb_ref[x] = b_ref[x] + b_ref[x + 2] + lane_neighbours(b_ref[x + 1], place & (NZ - 1), place)
        own = r_ref[x + 1]
        around = jnp.dot(own, near, preferred_element_type=f32)
        g = 6.0 * own.astype(f32) - around - r_ref[x].astype(f32) - r_ref[x + 2].astype(f32)
        g_ref[x] = g.astype(bf16)

    def block(ib, _):
        rows = pl.ds(pl.multiple_of(ib * IB, IB), IB)
        for s in range(6):
            u = jnp.dot(mix_ref[ib], r_ref[s], preferred_element_type=f32).reshape(NF, IB, CELLS)
            total = b_ref[s, 0:1] * u[0]
            for l in range(1, NF):
                total = total + b_ref[s, l : l + 1] * u[l]
            s_ref[s, rows] = total
            if 1 <= s <= 4:
                v = jnp.dot(mix_ref[ib], g_ref[s - 1], preferred_element_type=f32).reshape(NF, IB, CELLS)
                total = b_ref[s, 0:1] * v[0] + nb_ref[s - 1, 0:1] * u[0]
                for l in range(1, NF):
                    total = total + b_ref[s, l : l + 1] * v[l] + nb_ref[s - 1, l : l + 1] * u[l]
                t_ref[s - 1, rows] = total
        return 0

    lax.fori_loop(0, NIB, block, 0)
    for x in range(4):
        own = s_ref[x + 1]
        high = own.astype(bf16)
        low = (own - high.astype(f32)).astype(bf16)
        around = jnp.dot(high, near, preferred_element_type=f32) + jnp.dot(low, near, preferred_element_type=f32)
        out_ref[x] = (t_ref[x] - around - s_ref[x] - s_ref[x + 2]).astype(bf16)


def fill_faces(c0_ref, w_ref, inv_ref):
    place = iota((32, CELLS), 1)
    z_place = place & (NZ - 1)
    c = c0_ref[1]
    w_ref[0] = 0.5 * (c + c0_ref[2])
    w_ref[1] = 0.5 * (c + c0_ref[0])
    diag = w_ref[0] + w_ref[1]
    tests = ((CELLS - NZ, place < CELLS - NZ), (NZ, place >= NZ), (CELLS - 1, z_place < NZ - 1), (1, z_place > 0))
    for f, (amount, inside) in enumerate(tests):
        w = 0.5 * (c + jnp.where(inside, pltpu.roll(c, amount, 1), 0.0))
        diag = diag + w
        w_ref[2 + f] = jnp.where(inside, w, 0.0)
    inv_ref[...] = 1.0 / diag


def residual_kernel(img_ref, src_ref, c0_ref, res_ref, edge_ref, w_ref, inv_ref):
    fill_faces(c0_ref, w_ref, inv_ref)
    swap = swap_matrix(16, 32)
    for g in range(2):
        block = img_ref[:, 16 * g : 16 * (g + 1), :].reshape(512, CELLS)
        turned = jnp.dot(swap, block, preferred_element_type=f32).reshape(16, 32, CELLS)
        res_ref[16 * g : 16 * (g + 1)] = src_ref[16 * g : 16 * (g + 1)] - turned
    first_inv = inv_ref[...] * (1.0 / cheb_center)
    edge_ref[0] = res_ref[:, 0, :] * first_inv[0:1]
    edge_ref[1] = res_ref[:, 31, :] * first_inv[31:32]


def update_kernel(it_ref, res_ref, c0_ref, halo_ref, out_ref, w_ref, inv_ref):
    fill_faces(c0_ref, w_ref, inv_ref)
    row = iota((32, CELLS), 0)

    def one(mode, _):
        res = res_ref[mode]
        inv = inv_ref[...]
        first = res * inv * (1.0 / cheb_center)
        above = jnp.where(row == 31, halo_ref[1, pl.ds(mode, 1), :], pltpu.roll(first, 31, 0))
        below = jnp.where(row == 0, halo_ref[0, pl.ds(mode, 1), :], pltpu.roll(first, 1, 0))
        around = w_ref[0] * above + w_ref[1] * below
        for f, amount in enumerate((CELLS - NZ, NZ, CELLS - 1, 1)):
            around = around + w_ref[2 + f] * pltpu.roll(first, amount, 1)
        smoothed = res * (1.0 - 1.0 / cheb_center) + around
        second = rho_one * rho_zero * first + (2.0 * rho_one / cheb_radius) * smoothed * inv
        out_ref[mode] = it_ref[mode] + first + second
        return 0

    lax.fori_loop(0, 32, one, 0)


VM = pl.BlockSpec(memory_space=pltpu.VMEM)


def call(kernel, outs, ins, scratch):
    return pl.pallas_call(
        kernel,
        out_shape=outs,
        in_specs=[VM] * ins,
        out_specs=jax.tree.map(lambda _: VM, outs),
        scratch_shapes=scratch,
        compiler_params=pltpu.CompilerParams(vmem_limit_bytes=60 * 2**20),
    )


def swap_edges(low_side, high_side, axis):
    count = lax.axis_size(axis)
    forward = [(i, i + 1) for i in range(count - 1)]
    backward = [(b, a) for a, b in forward]
    return lax.ppermute(high_side, axis, forward), lax.ppermute(low_side, axis, backward)


def body(iterate, source, mean_coef, kl_fields, tri_index, tri_value):
    sds = jax.ShapeDtypeStruct
    mix, rows = call(
        prepare_kernel,
        (sds((NIB, NF * IB, P_SIZE), bf16), sds((32, 32, CELLS), bf16)),
        3,
        [pltpu.VMEM((P_SIZE, 64), f32)],
    )(tri_index.T, tri_value[None], iterate)
    coef = jnp.concatenate([mean_coef[None], kl_fields], 0)
    low, high = swap_edges(coef[:, :1], coef[:, -1:], "dom")
    coef = jnp.concatenate([low, coef, high], 1)
    c0 = jnp.stack([coef[0, 0:32], coef[0, 1:33], coef[0, 2:34]])
    low, high = swap_edges(rows[:1], rows[-1:], "dom")
    rows = jnp.concatenate([low, rows, high], 0)
    group = lax.axis_index("mode")
    mine = 0.5 * lax.dynamic_slice_in_dim(coef, group * 4, 6, 1)
    beta = jnp.pad(jnp.swapaxes(mine, 0, 1), ((0, 0), (0, 24 - NF), (0, 0)))
    windows = jnp.stack([rows[4 * d : 4 * d + 6] for d in range(8)])
    got = lax.all_to_all(windows, "mode", 0, 0, tiled=True)
    panel = jnp.swapaxes(got, 0, 1).reshape(6, P_SIZE, CELLS)
    image = call(
        image_kernel,
        sds((4, P_SIZE, CELLS), bf16),
        3,
        [
            pltpu.VMEM((4, P_SIZE, CELLS), bf16),
            pltpu.VMEM((4, 24, CELLS), f32),
            pltpu.VMEM((6, P_SIZE, CELLS), f32),
            pltpu.VMEM((4, P_SIZE, CELLS), f32),
        ],
    )(panel, mix, beta)
    back = jnp.swapaxes(image.reshape(4, 8, 32, CELLS), 0, 1)
    back = lax.all_to_all(back, "mode", 0, 0, tiled=True).reshape(32, 32, CELLS)
    faces = [pltpu.VMEM((6, 32, CELLS), f32), pltpu.VMEM((32, CELLS), f32)]
    block = sds((32, 32, CELLS), f32)
    residual, edges = call(residual_kernel, (block, sds((2, 32, CELLS), f32)), 3, faces)(back, source, c0)
    low, high = swap_edges(edges[0], edges[1], "dom")
    updated = call(update_kernel, block, 4, faces)(iterate, residual, c0, jnp.stack([low, high]))
    return updated, residual


def solution(mesh):
    return jax.shard_map(
        body,
        mesh=mesh,
        in_specs=(
            P("mode", "dom", None),
            P("mode", "dom", None),
            P("dom", None),
            P(None, "dom", None),
            P(),
            P(),
        ),
        out_specs=(P("mode", "dom", None), P("mode", "dom", None)),
        check_vma=False,
    )
```

time: 383 us -> 127 us (0.33)
  the two profiles are of different devices: /device:TPU:6 before, /device:TPU:26 now
where the time goes in v1:
time: 127 us; the launch traced here: 126 us
  starting transfers between devices  39.6 us (31%)
  waiting for transfers between devices  35.4 us (28%)
  Pallas kernels  29.5 us (23%)
  local copies, waits for them, and re-layouts  16.5 us (13%)
  other arithmetic  4.49 us (4%)
    ppermute x3, starting transfers between devices, swap_edges(): lax.ppermute(high_side, axis, forward)  25 us
    ppermute x3, waiting for transfers between devices, swap_edges(): lax.ppermute(low_side, axis, backward)  18 us
    all_to_all x1, waiting for transfers between devices, body(): back = lax.all_to_all(back, 'mode', 0, 0, tiled=True).reshape(32, 32, CELLS)  14.7 us
    pallas_call x1, Pallas kernels, body(): call(image_kernel, sds((4, P_SIZE, CELLS), bf16), 3, [pltpu.VMEM((4, P_SI...  12.2 us
    unnamed x13, local copies, waits for them, and re-layouts  10.1 us
    pallas_call x1, Pallas kernels, body(): call(prepare_kernel, (sds((NIB, NF * IB, P_SIZE), bf16), sds((32, 32, CEL...  8.2 us
    pallas_call x1, Pallas kernels, body(): call(update_kernel, block, 4, faces)  6.34 us
    ppermute x3, starting transfers between devices, swap_edges(): lax.ppermute(low_side, axis, backward)  5.76 us
  transfers between devices with their start and end apart: 8, of which 4 were waited for; matrix products, arithmetic and copies ran while one was open for 10% of the time, Pallas kernels for 0%

profile of v1, /device:TPU:26, one launch (start us, length us, event | category | flops | bytes accessed | tf_op | source)
XLA Modules:
  0.0 126.3 jit_solution(3150379253682943310)
XLA Ops:
  0.6 0.0 copy-start.2
  0.6 0.0 copy-start
  0.7 1.4 %broadcast_in_dim.6.val_ref = f32[1,5376]{1,0:T(1,128)} reshape(f32[5376]{0:T(1024)} %param.11) | data formatting | bytes 43008 | tf_op jit(solution)/shard_map/broadcast_in_dim | solution.py:200
  2.1 8.2 %shard_map.77 = (bf16[8,672,256]{2,1,0:T(8,128)(2,1)}, bf16[32,32,256]{2,1,0:T(8,128)(2,1)}) custom-call(s32[3,5376]{1,0:T(4,128)} %bitcast.44, f32[1,5376]{1,0:T(1,128)} %broadcast_in_dim.6.val_ref, f32[32,32,256]{2,1,0:T(8,128)} %it_ref.3), custom_call_target="tpu_custom_call" | custom-call | tf_op jit(solution)/shard_map/pallas_call | solution.py:195
  10.3 0.7 fusion.13
  11.0 8.7 %collective-permute-start = (bf16[1,32,256]{2,1,0:T(8,128)(2,1)S(1)}, bf16[1,32,256]{2,1,0:T(8,128)(2,1)S(1)}, u32[]{:S(2)}, u32[]{:S(2)}) collective-permute-start(bf16[1,32,256]{2,1,0:T(8,128)(2,1)S(1)} %get-tuple-element.13), channel_id=1, source_target_pairs={{0,8},{8,16},{16,24},{24,32},{32,40},{40,48},{48,56},{56,64},{64,7... | collective-permute-start | bytes 49160 | tf_op jit(solution)/shard_map/ppermute | solution.py:190
  19.8 1.9 %collective-permute-start.1 = (bf16[1,32,256]{2,1,0:T(8,128)(2,1)S(1)}, bf16[1,32,256]{2,1,0:T(8,128)(2,1)S(1)}, u32[]{:S(2)}, u32[]{:S(2)}) collective-permute-start(bf16[1,32,256]{2,1,0:T(8,128)(2,1)S(1)} %get-tuple-element.12), channel_id=1, source_target_pairs={{8,0},{16,8},{24,16},{32,24},{40,32},{48,40},{56,48},{64,56},{72,6... | collective-permute-start | bytes 49160 | tf_op jit(solution)/shard_map/ppermute | solution.py:190
  21.7 0.0 collective-permute-done
  21.7 1.5 %fusion.12 = bf16[8,6,32,256]{3,2,1,0:T(8,128)(2,1)} fusion(bf16[32,32,256]{2,1,0:T(8,128)(2,1)} %get-tuple-element.6, bf16[1,32,256]{2,1,0:T(8,128)(2,1)S(1)} %collective-permute-done), kind=kLoop, calls=%fused_computation.23 | loop fusion | flops 196607 | bytes 638976
  23.2 1.5 %bitcast_dynamic-update-slice_fusion.5 = bf16[8,6,32,256]{3,2,1,0:T(8,128)(2,1)} fusion(bf16[8,6,32,256]{3,2,1,0:T(8,128)(2,1)} %fusion.12, bf16[32,32,256]{2,1,0:T(8,128)(2,1)} %get-tuple-element.6), kind=kLoop, calls=%fused_computation.29 | loop fusion | bytes 196608
  24.8 1.5 %bitcast_dynamic-update-slice_fusion.4 = bf16[8,6,32,256]{3,2,1,0:T(8,128)(2,1)} fusion(bf16[8,6,32,256]{3,2,1,0:T(8,128)(2,1)} %bitcast_dynamic-update-slice_fusion.5, bf16[32,32,256]{2,1,0:T(8,128)(2,1)} %get-tuple-element.6), kind=kLoop, calls=%fused_computation.28 | loop fusion | bytes 196608
  26.3 1.5 %bitcast_dynamic-update-slice_fusion.3 = bf16[8,6,32,256]{3,2,1,0:T(8,128)(2,1)} fusion(bf16[8,6,32,256]{3,2,1,0:T(8,128)(2,1)} %bitcast_dynamic-update-slice_fusion.4, bf16[32,32,256]{2,1,0:T(8,128)(2,1)} %get-tuple-element.6), kind=kLoop, calls=%fused_computation.27 | loop fusion | bytes 196608
  27.9 1.5 %bitcast_dynamic-update-slice_fusion.2 = bf16[8,6,32,256]{3,2,1,0:T(8,128)(2,1)} fusion(bf16[8,6,32,256]{3,2,1,0:T(8,128)(2,1)} %bitcast_dynamic-update-slice_fusion.3, bf16[32,32,256]{2,1,0:T(8,128)(2,1)} %get-tuple-element.6), kind=kLoop, calls=%fused_computation.26 | loop fusion | bytes 196608
  29.4 1.5 %bitcast_dynamic-update-slice_fusion.1 = bf16[8,6,32,256]{3,2,1,0:T(8,128)(2,1)} fusion(bf16[8,6,32,256]{3,2,1,0:T(8,128)(2,1)} %bitcast_dynamic-update-slice_fusion.2, bf16[32,32,256]{2,1,0:T(8,128)(2,1)} %get-tuple-element.6), kind=kLoop, calls=%fused_computation.25 | loop fusion | bytes 196608
  30.9 1.5 %bitcast_dynamic-update-slice_fusion = bf16[8,6,32,256]{3,2,1,0:T(8,128)(2,1)} fusion(bf16[8,6,32,256]{3,2,1,0:T(8,128)(2,1)} %bitcast_dynamic-update-slice_fusion.1, bf16[32,32,256]{2,1,0:T(8,128)(2,1)} %get-tuple-element.6), kind=kLoop, calls=%fused_computation.24 | loop fusion | bytes 196608
  32.5 0.0 collective-permute-done.1
  32.5 1.5 %fusion.10 = bf16[8,6,32,256]{3,2,1,0:T(8,128)(2,1)} fusion(bf16[8,6,32,256]{3,2,1,0:T(8,128)(2,1)} %bitcast_dynamic-update-slice_fusion, bf16[1,32,256]{2,1,0:T(8,128)(2,1)S(1)} %collective-permute-done.1, bf16[32,32,256]{2,1,0:T(8,128)(2,1)} %get-tuple-element.6), kind=kLoop, calls=%fused_computation.20 | loop fusion | flops 196608 | bytes 638976 | tf_op jit(solution)/shard_map/stack | solution.py:210
  34.0 3.5 %all-to-all-start = ((bf16[8,6,32,256]{3,2,1,0:T(8,128)(2,1)}), bf16[8,6,32,256]{3,2,1,0:T(8,128)(2,1)S(1)}, u32[]{:S(2)}, u32[]{:S(2)}) async-start(bf16[8,6,32,256]{3,2,1,0:T(8,128)(2,1)} %fusion.10), calls=%async_computation | async-start | bytes 1572864 | tf_op jit(solution)/shard_map/all_to_all | solution.py:211
  37.6 0.0 copy-done.2
  37.6 0.0 copy-done
  37.6 9.9 %collective-permute-start.2 = (f32[21,1,256]{2,1,0:T(1,128)S(1)}, f32[21,1,256]{2,1,0:T(1,128)S(1)}, u32[]{:S(2)}, u32[]{:S(2)}) collective-permute-start(f32[21,1,256]{2,1,0:T(1,128)S(1)} %get-tuple-element.11), channel_id=1, source_target_pairs={{0,8},{8,16},{16,24},{24,32},{32,40},{40,48},{48,56},{56,64},{64,7... | collective-permute-start | bytes 64520 | tf_op jit(solution)/shard_map/ppermute | solution.py:190
  47.6 1.9 %collective-permute-start.3 = (f32[21,1,256]{2,1,0:T(1,128)S(1)}, f32[21,1,256]{2,1,0:T(1,128)S(1)}, u32[]{:S(2)}, u32[]{:S(2)}) collective-permute-start(f32[21,1,256]{2,1,0:T(1,128)S(1)} %get-tuple-element.10), channel_id=1, source_target_pairs={{8,0},{16,8},{24,16},{32,24},{40,32},{48,40},{56,48},{64,56},{72,6... | collective-permute-start | bytes 64520 | tf_op jit(solution)/shard_map/ppermute | solution.py:190
  49.5 2.7 %collective-permute-done.2 = f32[21,1,256]{2,1,0:T(1,128)S(1)} collective-permute-done((f32[21,1,256]{2,1,0:T(1,128)S(1)}, f32[21,1,256]{2,1,0:T(1,128)S(1)}, u32[]{:S(2)}, u32[]{:S(2)}) %collective-permute-start.2) | collective-permute-done | bytes 21536 | tf_op jit(solution)/shard_map/ppermute | solution.py:190
  52.3 8.0 %collective-permute-done.3 = f32[21,1,256]{2,1,0:T(1,128)S(1)} collective-permute-done((f32[21,1,256]{2,1,0:T(1,128)S(1)}, f32[21,1,256]{2,1,0:T(1,128)S(1)}, u32[]{:S(2)}, u32[]{:S(2)}) %collective-permute-start.3) | collective-permute-done | bytes 21536 | tf_op jit(solution)/shard_map/ppermute | solution.py:190
  60.3 0.1 fusion.3
  60.5 0.7 pad.4.clone.b_ref
  61.1 0.0 all-to-all-done
  61.1 0.9 copy.8
  62.1 12.2 %shard_map.78 = bf16[4,256,256]{2,1,0:T(8,128)(2,1)} custom-call(bf16[6,256,256]{2,1,0:T(8,128)(2,1)} %bitcast.37, bf16[8,672,256]{2,1,0:T(8,128)(2,1)} %get-tuple-element.7.mix_ref, f32[6,24,256]{2,1,0:T(8,128)} %pad.4.clone.b_ref), custom_call_target="tpu_custom_call" | custom-call | tf_op jit(solution)/shard_map/pallas_call | solution.py:213
  74.3 1.9 %copy.13 = bf16[4,8,32,256]{3,2,0,1:T(8,128)(2,1)} copy(bf16[4,8,32,256]{3,2,1,0:T(8,128)(2,1)} %bitcast.40) | data formatting | bytes 1048576 | tf_op jit(solution)/shard_map/reshape | solution.py:224
  76.2 5.2 %all-to-all-start.1 = ((bf16[8,4,32,256]{3,2,1,0:T(8,128)(2,1)}), bf16[8,4,32,256]{3,2,1,0:T(8,128)(2,1)S(1)}, u32[]{:S(2)}, u32[]{:S(2)}) async-start(bf16[8,4,32,256]{3,2,1,0:T(8,128)(2,1)} %bitcast.36), calls=%async_computation.1 | async-start | bytes 1048576 | tf_op jit(solution)/shard_map/all_to_all | solution.py:225
  81.4 0.7 fusion.5.c0_ref
  82.0 14.7 %all-to-all-done.1 = bf16[8,4,32,256]{3,2,1,0:T(8,128)(2,1)S(1)} async-done(((bf16[8,4,32,256]{3,2,1,0:T(8,128)(2,1)}), bf16[8,4,32,256]{3,2,1,0:T(8,128)(2,1)S(1)}, u32[]{:S(2)}, u32[]{:S(2)}) %all-to-all-start.1) | async-done | bytes 524320 | tf_op jit(solution)/shard_map/all_to_all | solution.py:225
  96.7 0.0 copy-start.1
  96.7 0.8 copy-done.1
  97.5 2.8 %shard_map.79 = (f32[32,32,256]{2,1,0:T(8,128)}, f32[2,32,256]{2,1,0:T(8,128)}) custom-call(bf16[32,32,256]{2,1,0:T(8,128)(2,1)} %bitcast.39, f32[32,32,256]{2,1,0:T(8,128)} %src_ref.1, f32[3,32,256]{2,1,0:T(8,128)} %fusion.5.c0_ref), custom_call_target="tpu_custom_call" | custom-call | tf_op jit(solution)/shard_map/pallas_call | solution.py:228
  100.3 0.8 slice_bitcast_fusion.1
  101.1 6.4 %collective-permute-start.4 = (f32[32,256]{1,0:T(8,128)S(1)}, f32[32,256]{1,0:T(8,128)S(1)}, u32[]{:S(2)}, u32[]{:S(2)}) collective-permute-start(f32[32,256]{1,0:T(8,128)S(1)} %get-tuple-element.14), channel_id=1, source_target_pairs={{0,8},{8,16},{16,24},{24,32},{32,40},{40,48},{48,56},{56,64},{64,7... | collective-permute-start | bytes 98312 | tf_op jit(solution)/shard_map/ppermute | solution.py:190
  107.4 1.9 %collective-permute-start.5 = (f32[32,256]{1,0:T(8,128)S(1)}, f32[32,256]{1,0:T(8,128)S(1)}, u32[]{:S(2)}, u32[]{:S(2)}) collective-permute-start(f32[32,256]{1,0:T(8,128)S(1)} %get-tuple-element.15), channel_id=1, source_target_pairs={{8,0},{16,8},{24,16},{32,24},{40,32},{48,40},{56,48},{64,56},{72,6... | collective-permute-start | bytes 98312 | tf_op jit(solution)/shard_map/ppermute | solution.py:190
  109.4 0.0 collective-permute-done.4
  109.4 9.9 %collective-permute-done.5 = f32[32,256]{1,0:T(8,128)S(1)} collective-permute-done((f32[32,256]{1,0:T(8,128)S(1)}, f32[32,256]{1,0:T(8,128)S(1)}, u32[]{:S(2)}, u32[]{:S(2)}) %collective-permute-start.5) | collective-permute-done | bytes 32800 | tf_op jit(solution)/shard_map/ppermute | solution.py:190
  119.3 0.6 pad_maximum_fusion.4.halo_ref
  119.9 6.3 %shard_map.80 = f32[32,32,256]{2,1,0:T(8,128)} custom-call(f32[32,32,256]{2,1,0:T(8,128)} %it_ref.3, f32[32,32,256]{2,1,0:T(8,128)} %get-tuple-element.5.res_ref, f32[3,32,256]{2,1,0:T(8,128)} %fusion.5.c0_ref, f32[2,32,256]{2,1,0:T(8,128)} %pad_maximum_fusion.4.halo_ref), custom_call_target="tpu_custom_call" | custom-call | tf_op jit(solution)/shard_map/pallas_call | solution.py:230
  (2 shorter events, 0.1 us)
Async XLA Ops:
  0.6 36.9 %copy-start.2 = (f32[32,256]{1,0:T(8,128)S(1)}, f32[32,256]{1,0:T(8,128)}, u32[]{:S(2)}) copy-start(f32[32,256]{1,0:T(8,128)} %param.8) | copy-start | bytes 98308
  0.6 36.9 %copy-start = (f32[20,32,256]{2,1,0:T(8,128)S(1)}, f32[20,32,256]{2,1,0:T(8,128)}, u32[]{:S(2)}) copy-start(f32[20,32,256]{2,1,0:T(8,128)} %param.9) | copy-start | bytes 1966084
  11.0 10.7 %collective-permute-start = (bf16[1,32,256]{2,1,0:T(8,128)(2,1)S(1)}, bf16[1,32,256]{2,1,0:T(8,128)(2,1)S(1)}, u32[]{:S(2)}, u32[]{:S(2)}) collective-permute-start(bf16[1,32,256]{2,1,0:T(8,128)(2,1)S(1)} %get-tuple-element.13), channel_id=1, source_target_pairs={{0,8},{8,16},{16,24},{24,32},{32,40},{40,48},{48,56},{56,64},{64,7... | collective-permute-start | bytes 49160 | tf_op jit(solution)/shard_map/ppermute | solution.py:190
  19.8 12.7 %collective-permute-start.1 = (bf16[1,32,256]{2,1,0:T(8,128)(2,1)S(1)}, bf16[1,32,256]{2,1,0:T(8,128)(2,1)S(1)}, u32[]{:S(2)}, u32[]{:S(2)}) collective-permute-start(bf16[1,32,256]{2,1,0:T(8,128)(2,1)S(1)} %get-tuple-element.12), channel_id=1, source_target_pairs={{8,0},{16,8},{24,16},{32,24},{40,32},{48,40},{56,48},{64,56},{72,6... | collective-permute-start | bytes 49160 | tf_op jit(solution)/shard_map/ppermute | solution.py:190
  34.0 27.1 %all-to-all-start = ((bf16[8,6,32,256]{3,2,1,0:T(8,128)(2,1)}), bf16[8,6,32,256]{3,2,1,0:T(8,128)(2,1)S(1)}, u32[]{:S(2)}, u32[]{:S(2)}) async-start(bf16[8,6,32,256]{3,2,1,0:T(8,128)(2,1)} %fusion.10), calls=%async_computation | async-start | bytes 1572864 | tf_op jit(solution)/shard_map/all_to_all | solution.py:211
  37.6 14.6 %collective-permute-start.2 = (f32[21,1,256]{2,1,0:T(1,128)S(1)}, f32[21,1,256]{2,1,0:T(1,128)S(1)}, u32[]{:S(2)}, u32[]{:S(2)}) collective-permute-start(f32[21,1,256]{2,1,0:T(1,128)S(1)} %get-tuple-element.11), channel_id=1, source_target_pairs={{0,8},{8,16},{16,24},{24,32},{32,40},{40,48},{48,56},{56,64},{64,7... | collective-permute-start | bytes 64520 | tf_op jit(solution)/shard_map/ppermute | solution.py:190
  47.6 12.7 %collective-permute-start.3 = (f32[21,1,256]{2,1,0:T(1,128)S(1)}, f32[21,1,256]{2,1,0:T(1,128)S(1)}, u32[]{:S(2)}, u32[]{:S(2)}) collective-permute-start(f32[21,1,256]{2,1,0:T(1,128)S(1)} %get-tuple-element.10), channel_id=1, source_target_pairs={{8,0},{16,8},{24,16},{32,24},{40,32},{48,40},{56,48},{64,56},{72,6... | collective-permute-start | bytes 64520 | tf_op jit(solution)/shard_map/ppermute | solution.py:190
  76.2 20.5 %all-to-all-start.1 = ((bf16[8,4,32,256]{3,2,1,0:T(8,128)(2,1)}), bf16[8,4,32,256]{3,2,1,0:T(8,128)(2,1)S(1)}, u32[]{:S(2)}, u32[]{:S(2)}) async-start(bf16[8,4,32,256]{3,2,1,0:T(8,128)(2,1)} %bitcast.36), calls=%async_computation.1 | async-start | bytes 1048576 | tf_op jit(solution)/shard_map/all_to_all | solution.py:225
  96.7 0.8 copy-start.1
  101.1 8.3 %collective-permute-start.4 = (f32[32,256]{1,0:T(8,128)S(1)}, f32[32,256]{1,0:T(8,128)S(1)}, u32[]{:S(2)}, u32[]{:S(2)}) collective-permute-start(f32[32,256]{1,0:T(8,128)S(1)} %get-tuple-element.14), channel_id=1, source_target_pairs={{0,8},{8,16},{16,24},{24,32},{32,40},{40,48},{48,56},{56,64},{64,7... | collective-permute-start | bytes 98312 | tf_op jit(solution)/shard_map/ppermute | solution.py:190
  107.4 11.9 %collective-permute-start.5 = (f32[32,256]{1,0:T(8,128)S(1)}, f32[32,256]{1,0:T(8,128)S(1)}, u32[]{:S(2)}, u32[]{:S(2)}) collective-permute-start(f32[32,256]{1,0:T(8,128)S(1)} %get-tuple-element.15), channel_id=1, source_target_pairs={{8,0},{16,8},{24,16},{32,24},{40,32},{48,40},{56,48},{64,56},{72,6... | collective-permute-start | bytes 98312 | tf_op jit(solution)/shard_map/ppermute | solution.py:190

commit v2 on v1

v2 whole, which is shorter than its diff:
```python
import jax
import jax.numpy as jnp
from jax import lax
from jax.experimental import pallas as pl
from jax.experimental.pallas import tpu as pltpu
from jax.sharding import PartitionSpec as P

P_SIZE = 256
NF = 21
NZ = 16
CELLS = 256
IB = 32
NIB = P_SIZE // IB
ENTRIES = P_SIZE * NF

cheb_center = 1.125
cheb_radius = 0.875
sigma = cheb_center / cheb_radius
rho_zero = 1.0 / sigma
rho_one = 1.0 / (2.0 * sigma - rho_zero)

f32 = jnp.float32
bf16 = jnp.bfloat16
i32 = jnp.int32


def iota(shape, dim):
    return lax.broadcasted_iota(i32, shape, dim)


def plane_neighbours():
    q = iota((CELLS, CELLS), 0)
    p = iota((CELLS, CELLS), 1)
    far = jnp.abs(q - p)
    same = (q >> 4) == (p >> 4)
    return jnp.where((far == NZ) | ((far == 1) & same), 1.0, 0.0).astype(bf16)


def build_mixing(tri_ref, val_ref, mix_ref, table_ref):
    mode = iota((P_SIZE, 256), 0)
    level = iota((32, 256), 0)

    def gather(step, total):
        here = pl.ds(pl.multiple_of(step * 256, 256), 256)
        worth = jnp.concatenate([val_ref[pl.ds(2 * step, 1)], val_ref[pl.ds(2 * step + 1, 1)]], 1)
        hot = jnp.where(mode == tri_ref[0:1, here], 1.0, 0.0).astype(bf16)
        mine = level == tri_ref[2:3, here]
        coef = jnp.where(mine, worth, 0.0).astype(bf16)
        trial = jnp.where(mine, tri_ref[1:2, here].astype(f32), 0.0).astype(bf16)
        both = jnp.concatenate([coef, trial], 0)
        return total + lax.dot_general(
            hot, both, (((1,), (1,)), ((), ())), preferred_element_type=f32
        )

    table_ref[...] = lax.fori_loop(0, ENTRIES // 256, gather, jnp.zeros((P_SIZE, 64), f32))
    column = iota((P_SIZE, P_SIZE), 1).astype(f32)
    for l in range(NF):
        coef = table_ref[:, l : l + 1]
        trial = table_ref[:, 32 + l : 33 + l]
        panel = jnp.where(column == trial, coef, 0.0).astype(bf16)
        mix_ref[:, l * IB : (l + 1) * IB, :] = panel.reshape(NIB, IB, P_SIZE)


def swap_matrix(major, minor):
    n = major * minor
    r = iota((n, n), 0)
    c = iota((n, n), 1)
    shift = minor.bit_length() - 1
    wanted = (r & (minor - 1)) * major + (r >> shift)
    return jnp.where(c == wanted, 1.0, 0.0).astype(bf16)


def lane_neighbours(x, z_place, place):
    up = jnp.where(z_place < NZ - 1, pltpu.roll(x, CELLS - 1, x.ndim - 1), 0.0)
    down = jnp.where(z_place > 0, pltpu.roll(x, 1, x.ndim - 1), 0.0)
    far = jnp.where(place < CELLS - NZ, pltpu.roll(x, CELLS - NZ, x.ndim - 1), 0.0)
    near = jnp.where(place >= NZ, pltpu.roll(x, NZ, x.ndim - 1), 0.0)
    return up + down + far + near


def fill_faces(c0_ref, w_ref, inv_ref):
    place = iota((32, CELLS), 1)
    z_place = place & (NZ - 1)
    c = c0_ref[1]
    w_ref[0] = 0.5 * (c + c0_ref[2])
    w_ref[1] = 0.5 * (c + c0_ref[0])
    diag = w_ref[0] + w_ref[1]
    tests = ((CELLS - NZ, place < CELLS - NZ), (NZ, place >= NZ), (CELLS - 1, z_place < NZ - 1), (1, z_place > 0))
    for f, (amount, inside) in enumerate(tests):
        w = 0.5 * (c + jnp.where(inside, pltpu.roll(c, amount, 1), 0.0))
        diag = diag + w
        w_ref[2 + f] = jnp.where(inside, w, 0.0)
    inv_ref[...] = 1.0 / diag


MESH = pl.DeviceIdType.MESH
GROUP = 8


def row_of(device, k):
    core = lax.rem(device, 2)
    return 8 * (device // 2) + core * (3 + k) + (1 - core) * (4 - k)


def fused_kernel(
    it_hbm, src_hbm, mean_ref, kl_hbm, tri_ref, val_ref, upd_ref, res_ref,
    it_ref, src_ref, kl_ref, rows_ref, edge_ref, r_ref, mix_ref, table_ref, g_ref, b_ref, nb_ref, s_ref, t_ref,
    ce_ref, ch_ref, out_ref, img_ref, fe_ref, fh_ref, c0_ref, w_ref, inv_ref,
    local_sem, edge_sem, send_sem, recv_sem, coef_sem, back_sem, home_sem, first_sem,
):
    d = lax.axis_index("dom")
    m = lax.axis_index("mode")
    count = lax.axis_size("dom")
    up = lax.rem(d + 1, count)
    down = lax.rem(d + count - 1, count)
    sibling = m + 1 - 2 * lax.rem(m, 2)
    peers = [lax.rem(m + p, GROUP) for p in range(1, GROUP)]
    own_modes = pl.ds(pl.multiple_of(m * 32, 32), 32)

    def send(source, target, device, sent, got):
        copy = pltpu.make_async_remote_copy(
            src_ref=source, dst_ref=target, send_sem=sent, recv_sem=got, device_id=device, device_id_type=MESH
        )
        copy.start()
        return copy

    def drain(ref, sem):
        pltpu.make_async_copy(ref, ref, sem).wait()

    loads = [
        pltpu.make_async_copy(a, b, local_sem.at[i])
        for i, (a, b) in enumerate(((it_hbm, it_ref), (kl_hbm, kl_ref), (src_hbm, src_ref)))
    ]
    for load in loads:
        load.start()
    barrier = pltpu.get_barrier_semaphore()
    for peer in peers:
        pl.semaphore_signal(barrier, inc=1, device_id=(d, peer), device_id_type=MESH)
    for other in (up, down):
        pl.semaphore_signal(barrier, inc=1, device_id=(other, m), device_id_type=MESH)

    loads[0].wait()
    swap = swap_matrix(32, 16)
    for g in range(2):
        block = it_ref[16 * g : 16 * (g + 1)].astype(bf16).reshape(512, CELLS)
        turned = jnp.dot(swap, block, preferred_element_type=f32).astype(bf16)
        rows_ref[:, 16 * g : 16 * (g + 1), :] = turned.reshape(32, 16, CELLS)
    loads[1].wait()
    blank = jnp.zeros((3, CELLS), f32)
    for side, row in ((0, 0), (1, 31)):
        ce_ref[side] = jnp.concatenate([mean_ref[row : row + 1], kl_ref[:, row, :], blank], 0)
    pl.semaphore_wait(barrier, GROUP + 1)

    edges = [
        send(rows_ref.at[31], edge_ref.at[0], (up, m), edge_sem.at[0], edge_sem.at[2]),
        send(rows_ref.at[0], edge_ref.at[1], (down, m), edge_sem.at[1], edge_sem.at[3]),
    ]
    coefs = [
        send(ce_ref.at[1], ch_ref.at[0], (up, m), coef_sem.at[0], coef_sem.at[2]),
        send(ce_ref.at[0], ch_ref.at[1], (down, m), coef_sem.at[1], coef_sem.at[3]),
    ]
    for k in range(1, 6):
        for peer in peers:
            row = row_of(peer, k)

            def pass_row():
                send(rows_ref.at[row], r_ref.at[k, own_modes], (d, peer), send_sem.at[k], recv_sem.at[k])

            if k < 5:
                pass_row()
            else:
                pl.when((row >= 0) & (row < 32))(pass_row)
        row = row_of(m, k)

        def keep_row():
            pltpu.make_async_copy(rows_ref.at[row], r_ref.at[k, own_modes], recv_sem.at[k]).start()

        if k < 5:
            keep_row()
        else:
            pl.when((row >= 0) & (row < 32))(keep_row)

    build_mixing(tri_ref, val_ref, mix_ref, table_ref)

    for side, holder in ((0, 0), (1, GROUP - 1)):
        edges[side].wait_recv()

        @pl.when(m == holder)
        def _():
            pltpu.make_async_copy(edge_ref.at[side], r_ref.at[5, own_modes], recv_sem.at[5]).start()

        @pl.when(m != holder)
        def _():
            send(edge_ref.at[side], r_ref.at[5, own_modes], (d, holder), send_sem.at[5], recv_sem.at[5])

    for copy in coefs:
        copy.wait_recv()
    first_edge = jnp.where(d == 0, 0.0, 1.0)
    last_edge = jnp.where(d == count - 1, 0.0, 1.0)
    outer = jnp.where(m == 0, first_edge, jnp.where(m == GROUP - 1, last_edge, 1.0))
    b_ref[...] = jnp.zeros_like(b_ref)
    for k in range(6):
        row = row_of(m, k)
        if k == 5:
            row = jnp.minimum(jnp.maximum(row, 0), 31)
        mean_row = mean_ref[pl.ds(row, 1), :]
        kl_row = kl_ref[:, pl.ds(row, 1), :].reshape(NF - 1, CELLS)
        here = jnp.concatenate([mean_row, kl_row, blank], 0)
        if k == 5:
            here = jnp.where(m == 0, ch_ref[0], jnp.where(m == GROUP - 1, ch_ref[1], here)) * outer
        b_ref[k] = 0.5 * here
    place = iota((24, CELLS), 1)
    for k in range(1, 5):
        nb_ref[k - 1] = b_ref[k - 1] + b_ref[k + 1] + lane_neighbours(b_ref[k], place & (NZ - 1), place)

    row = iota((32, CELLS), 0)
    mean = mean_ref[...]
    c0_ref[0] = jnp.where(row == 0, ch_ref[0, 0:1] * first_edge, pltpu.roll(mean, 1, 0))
    c0_ref[1] = mean
    c0_ref[2] = jnp.where(row == 31, ch_ref[1, 0:1] * last_edge, pltpu.roll(mean, 31, 0))
    fill_faces(c0_ref, w_ref, inv_ref)
    near = plane_neighbours()

    def mix_slot(k):
        def block(ib, _):
            rows = pl.ds(pl.multiple_of(ib * IB, IB), IB)
            u = jnp.dot(mix_ref[ib], r_ref[k], preferred_element_type=f32).reshape(NF, IB, CELLS)
            total = b_ref[k, 0:1] * u[0]
            for l in range(1, NF):
                total = total + b_ref[k, l : l + 1] * u[l]
            s_ref[k, rows] = total
            if 1 <= k <= 4:
                total = nb_ref[k - 1, 0:1] * u[0]
                for l in range(1, NF):
                    total = total + nb_ref[k - 1, l : l + 1] * u[l]
                t_ref[k - 1, rows] = total
            return 0

        lax.fori_loop(0, NIB, block, 0)

    def finish_row(k):
        own = r_ref[k]
        ahead = r_ref[k + 1].astype(f32)
        if k == 4:
            ahead = ahead * outer
        around = jnp.dot(own, near, preferred_element_type=f32)
        g_ref[...] = (6.0 * own.astype(f32) - around - r_ref[k - 1].astype(f32) - ahead).astype(bf16)

        def block(ib, _):
            rows = pl.ds(pl.multiple_of(ib * IB, IB), IB)
            v = jnp.dot(mix_ref[ib], g_ref[...], preferred_element_type=f32).reshape(NF, IB, CELLS)
            total = t_ref[k - 1, rows]
            for l in range(NF):
                total = total + b_ref[k, l : l + 1] * v[l]
            t_ref[k - 1, rows] = total
            return 0

        lax.fori_loop(0, NIB, block, 0)
        own = s_ref[k]
        high = own.astype(bf16)
        low = (own - high.astype(f32)).astype(bf16)
        around = jnp.dot(high, near, preferred_element_type=f32) + jnp.dot(low, near, preferred_element_type=f32)
        out_ref[k - 1] = (t_ref[k - 1] - around - s_ref[k - 1] - s_ref[k + 1]).astype(bf16)
        row = row_of(m, k)
        for peer in peers:
            modes = pl.ds(pl.multiple_of(peer * 32, 32), 32)
            send(out_ref.at[k - 1, modes], img_ref.at[row], (d, peer), back_sem.at[k - 1], home_sem.at[k - 1])
        pltpu.make_async_copy(out_ref.at[k - 1, own_modes], img_ref.at[row], home_sem.at[k - 1]).start()

    drain(r_ref.at[1], recv_sem.at[1])
    forward = send(r_ref.at[1], r_ref.at[0], (d, sibling), send_sem.at[0], recv_sem.at[0])
    mix_slot(1)
    drain(r_ref.at[2], recv_sem.at[2])
    mix_slot(2)
    forward.wait_recv()
    mix_slot(0)
    finish_row(1)
    for k in range(2, 5):
        drain(r_ref.at[k + 1], recv_sem.at[k + 1])
        mix_slot(k + 1)
        finish_row(k)

    loads[2].wait()
    for k in range(4):
        drain(img_ref.at[0:8], home_sem.at[k])
    first_inv = inv_ref[...] * (1.0 / cheb_center)
    for side, row in ((0, 0), (1, 31)):
        fe_ref[side] = (src_ref[:, row, :] - img_ref[row].astype(f32)) * first_inv[row : row + 1]
    firsts = [
        send(fe_ref.at[1], fh_ref.at[0], (up, m), first_sem.at[0], first_sem.at[2]),
        send(fe_ref.at[0], fh_ref.at[1], (down, m), first_sem.at[1], first_sem.at[3]),
    ]
    swap = swap_matrix(16, 32)
    for g in range(2):
        block = img_ref[:, 16 * g : 16 * (g + 1), :].reshape(512, CELLS)
        turned = jnp.dot(swap, block, preferred_element_type=f32).reshape(16, 32, CELLS)
        res_ref[16 * g : 16 * (g + 1)] = src_ref[16 * g : 16 * (g + 1)] - turned
    for copy in firsts:
        copy.wait_recv()
    row = iota((32, CELLS), 0)

    def update(mode, _):
        res = res_ref[mode]
        inv = inv_ref[...]
        first = res * inv * (1.0 / cheb_center)
        above = jnp.where(row == 31, fh_ref[1, pl.ds(mode, 1), :] * last_edge, pltpu.roll(first, 31, 0))
        below = jnp.where(row == 0, fh_ref[0, pl.ds(mode, 1), :] * first_edge, pltpu.roll(first, 1, 0))
        around = w_ref[0] * above + w_ref[1] * below
        for f, amount in enumerate((CELLS - NZ, NZ, CELLS - 1, 1)):
            around = around + w_ref[2 + f] * pltpu.roll(first, amount, 1)
        smoothed = res * (1.0 - 1.0 / cheb_center) + around
        second = rho_one * rho_zero * first + (2.0 * rho_one / cheb_radius) * smoothed * inv
        upd_ref[mode] = it_ref[mode] + first + second
        return 0

    lax.fori_loop(0, 32, update, 0)

    for copy in edges + coefs + firsts + [forward]:
        copy.wait_send()
    sent = pl.ds(0, 32 * (GROUP - 1))
    for k in range(1, 6):
        drain(r_ref.at[k, sent], send_sem.at[k])
    for k in range(4):
        drain(out_ref.at[k, sent], back_sem.at[k])


def body(iterate, source, mean_coef, kl_fields, tri_index, tri_value):
    sds = jax.ShapeDtypeStruct
    vm = pl.BlockSpec(memory_space=pltpu.VMEM)
    anywhere = pl.BlockSpec(memory_space=pl.ANY)
    block = sds((32, 32, CELLS), f32)
    dma = pltpu.SemaphoreType.DMA
    return pl.pallas_call(
        fused_kernel,
        out_shape=(block, block),
        in_specs=[anywhere, anywhere, vm, anywhere, vm, vm],
        out_specs=(vm, vm),
        scratch_shapes=[
            pltpu.VMEM((32, 32, CELLS), f32),
            pltpu.VMEM((32, 32, CELLS), f32),
            pltpu.VMEM((NF - 1, 32, CELLS), f32),
            pltpu.VMEM((32, 32, CELLS), bf16),
            pltpu.VMEM((2, 32, CELLS), bf16),
            pltpu.VMEM((6, P_SIZE, CELLS), bf16),
            pltpu.VMEM((NIB, NF * IB, P_SIZE), bf16),
            pltpu.VMEM((P_SIZE, 64), f32),
            pltpu.VMEM((P_SIZE, CELLS), bf16),
            pltpu.VMEM((6, 24, CELLS), f32),
            pltpu.VMEM((4, 24, CELLS), f32),
            pltpu.VMEM((6, P_SIZE, CELLS), f32),
            pltpu.VMEM((4, P_SIZE, CELLS), f32),
            pltpu.VMEM((2, 24, CELLS), f32),
            pltpu.VMEM((2, 24, CELLS), f32),
            pltpu.VMEM((4, P_SIZE, CELLS), bf16),
            pltpu.VMEM((32, 32, CELLS), bf16),
            pltpu.VMEM((2, 32, CELLS), f32),
            pltpu.VMEM((2, 32, CELLS), f32),
            pltpu.VMEM((3, 32, CELLS), f32),
            pltpu.VMEM((6, 32, CELLS), f32),
            pltpu.VMEM((32, CELLS), f32),
            dma((3,)),
            dma((4,)),
            dma((6,)),
            dma((6,)),
            dma((4,)),
            dma((4,)),
            dma((4,)),
            dma((4,)),
        ],
        compiler_params=pltpu.CompilerParams(
            collective_id=0, has_side_effects=True, vmem_limit_bytes=60 * 2**20
        ),
    )(iterate, source, mean_coef, kl_fields, tri_index.T, tri_value.reshape(42, 128))


def solution(mesh):
    return jax.shard_map(
        body,
        mesh=mesh,
        in_specs=(
            P("mode", "dom", None),
            P("mode", "dom", None),
            P("dom", None),
            P(None, "dom", None),
            P(),
            P(),
        ),
        out_specs=(P("mode", "dom", None), P("mode", "dom", None)),
        check_vma=False,
    )
```

time: 127 us -> 67.1 us (0.53)
  the two profiles are of different devices: /device:TPU:26 before, /device:TPU:1 now
where the time goes in v2:
time: 67.1 us; the launch traced here: 66.9 us
  Pallas kernels  62.9 us (94%)
  local copies, waits for them, and re-layouts  3.37 us (5%)
    pallas_call x1, Pallas kernels, body(): pl.pallas_call(fused_kernel, out_shape=(block, block), in_specs=[anywhere...  62.9 us
    unnamed x4, local copies, waits for them, and re-layouts  3.37 us

profile of v2, /device:TPU:1, one launch (start us, length us, event | category | flops | bytes accessed | tf_op | source)
XLA Modules:
  0.0 66.9 jit_solution(16405973197879604877)
XLA Ops:
  0.6 62.9 %shard_map.77 = (f32[32,32,256]{2,1,0:T(8,128)}, f32[32,32,256]{2,1,0:T(8,128)}) custom-call(f32[32,32,256]{2,1,0:T(8,128)} %it_hbm.1, f32[32,32,256]{2,1,0:T(8,128)} %src_hbm.1, f32[32,256]{1,0:T(8,128)} %mean_ref.1, f32[20,32,256]{2,1,0:T(8,128)} %kl_hbm.1, s32[3,5376]{1,0:T(4,128)} %bitcast.2, f32[42,128]{1,0:T(8,128)} %bitcast.3), custom_call_target="tpu_custom_call" | custom-call | tf_op jit(solution)/shard_map/pallas_call | solution.py:333
  63.6 0.0 copy-start
  63.6 2.4 %copy.10 = f32[32,32,256]{2,1,0:T(8,128)} copy(f32[32,32,256]{2,1,0:T(8,128)} %get-tuple-element.4) | data formatting | bytes 2097152
  66.0 0.0 copy-done
  66.0 1.0 %copy.11 = f32[32,32,256]{2,1,0:T(8,128)} copy(f32[32,32,256]{2,1,0:T(8,128)S(1)} %copy-done) | data formatting | bytes 2097152
Async XLA Ops:
  63.6 2.4 %copy-start = (f32[32,32,256]{2,1,0:T(8,128)S(1)}, f32[32,32,256]{2,1,0:T(8,128)}, u32[]{:S(2)}) copy-start(f32[32,32,256]{2,1,0:T(8,128)} %get-tuple-element.5) | copy-start | bytes 3145732

commit v3 on v2

v3 whole, which is shorter than its diff:
```python
import jax
import jax.numpy as jnp
from jax import lax
from jax.experimental import pallas as pl
from jax.experimental.pallas import tpu as pltpu
from jax.sharding import PartitionSpec as P

P_SIZE = 256
NF = 21
NZ = 16
CELLS = 256
IB = 32
NIB = P_SIZE // IB
ENTRIES = P_SIZE * NF

cheb_center = 1.125
cheb_radius = 0.875
sigma = cheb_center / cheb_radius
rho_zero = 1.0 / sigma
rho_one = 1.0 / (2.0 * sigma - rho_zero)

f32 = jnp.float32
bf16 = jnp.bfloat16
i32 = jnp.int32


def iota(shape, dim):
    return lax.broadcasted_iota(i32, shape, dim)


def plane_neighbours():
    q = iota((CELLS, CELLS), 0)
    p = iota((CELLS, CELLS), 1)
    far = jnp.abs(q - p)
    same = (q >> 4) == (p >> 4)
    return jnp.where((far == NZ) | ((far == 1) & same), 1.0, 0.0).astype(bf16)


def fill_table(tri_ref, val_ref, table_ref):
    mode = iota((P_SIZE, 256), 0)
    level = iota((32, 256), 0)

    def gather(step, total):
        here = pl.ds(pl.multiple_of(step * 256, 256), 256)
        worth = jnp.concatenate([val_ref[pl.ds(2 * step, 1)], val_ref[pl.ds(2 * step + 1, 1)]], 1)
        hot = jnp.where(mode == tri_ref[0:1, here], 1.0, 0.0).astype(bf16)
        mine = level == tri_ref[2:3, here]
        coef = jnp.where(mine, worth, 0.0).astype(bf16)
        trial = jnp.where(mine, tri_ref[1:2, here].astype(f32), 0.0).astype(bf16)
        both = jnp.concatenate([coef, trial], 0)
        return total + lax.dot_general(
            hot, both, (((1,), (1,)), ((), ())), preferred_element_type=f32
        )

    table_ref[...] = lax.fori_loop(0, ENTRIES // 256, gather, jnp.zeros((P_SIZE, 64), f32))


def fill_mixing(table_ref, mix_ref):
    column = iota((P_SIZE, P_SIZE), 1).astype(f32)
    for l in range(NF):
        coef = table_ref[:, l : l + 1]
        trial = table_ref[:, 32 + l : 33 + l]
        panel = jnp.where(column == trial, coef, 0.0).astype(bf16)
        mix_ref[:, l * IB : (l + 1) * IB, :] = panel.reshape(NIB, IB, P_SIZE)


def swap_matrix(major, minor):
    n = major * minor
    r = iota((n, n), 0)
    c = iota((n, n), 1)
    shift = minor.bit_length() - 1
    wanted = (r & (minor - 1)) * major + (r >> shift)
    return jnp.where(c == wanted, 1.0, 0.0).astype(bf16)


def lane_neighbours(x, z_place, place):
    up = jnp.where(z_place < NZ - 1, pltpu.roll(x, CELLS - 1, x.ndim - 1), 0.0)
    down = jnp.where(z_place > 0, pltpu.roll(x, 1, x.ndim - 1), 0.0)
    far = jnp.where(place < CELLS - NZ, pltpu.roll(x, CELLS - NZ, x.ndim - 1), 0.0)
    near = jnp.where(place >= NZ, pltpu.roll(x, NZ, x.ndim - 1), 0.0)
    return up + down + far + near


def fill_faces(c0_ref, w_ref, inv_ref):
    place = iota((32, CELLS), 1)
    z_place = place & (NZ - 1)
    c = c0_ref[1]
    w_ref[0] = 0.5 * (c + c0_ref[2])
    w_ref[1] = 0.5 * (c + c0_ref[0])
    diag = w_ref[0] + w_ref[1]
    tests = ((CELLS - NZ, place < CELLS - NZ), (NZ, place >= NZ), (CELLS - 1, z_place < NZ - 1), (1, z_place > 0))
    for f, (amount, inside) in enumerate(tests):
        w = 0.5 * (c + jnp.where(inside, pltpu.roll(c, amount, 1), 0.0))
        diag = diag + w
        w_ref[2 + f] = jnp.where(inside, w, 0.0)
    inv_ref[...] = 1.0 / diag


MESH = pl.DeviceIdType.MESH
GROUP = 8


def row_of(device, k):
    core = lax.rem(device, 2)
    return 8 * (device // 2) + core * (8 - k) + (1 - core) * (k - 1)


def exchange_kernel(
    it_hbm, src_hbm, mean_hbm, kl_hbm, tri_hbm, val_hbm, nat_ref, halo_ref, w_ref, inv_ref,
    it_ref, src_ref, mean_ref, kl_ref, tri_ref, val_ref, rows_ref, edge_ref, r_ref, mix_ref, table_ref, g_ref, b_ref, nb_ref, s_ref, t_ref,
    ce_ref, ch_ref, out_ref, img_ref, fe_ref, fh_ref, c0_ref,
    local_sem, edge_sem, send_sem, recv_sem, coef_sem, back_sem, home_sem, first_sem,
):
    d = lax.axis_index("dom")
    m = lax.axis_index("mode")
    count = lax.axis_size("dom")
    up = lax.rem(d + 1, count)
    down = lax.rem(d + count - 1, count)
    sibling = m + 1 - 2 * lax.rem(m, 2)
    peers = [lax.rem(m + p, GROUP) for p in range(1, GROUP)]
    own_modes = pl.ds(pl.multiple_of(m * 32, 32), 32)

    def send(source, target, device, sent, got):
        copy = pltpu.make_async_remote_copy(
            src_ref=source, dst_ref=target, send_sem=sent, recv_sem=got, device_id=device, device_id_type=MESH
        )
        copy.start()
        return copy

    def drain(ref, sem):
        pltpu.make_async_copy(ref, ref, sem).wait()

    loads = [
        pltpu.make_async_copy(a, b, local_sem.at[i])
        for i, (a, b) in enumerate(
            (
                (it_hbm, it_ref),
                (kl_hbm, kl_ref),
                (mean_hbm, mean_ref),
                (tri_hbm, tri_ref),
                (val_hbm, val_ref),
                (src_hbm, src_ref),
            )
        )
    ]
    for load in loads:
        load.start()
    barrier = pltpu.get_barrier_semaphore()
    for peer in peers:
        pl.semaphore_signal(barrier, inc=1, device_id=(d, peer), device_id_type=MESH)
    for other in (up, down):
        pl.semaphore_signal(barrier, inc=1, device_id=(other, m), device_id_type=MESH)

    loads[0].wait()
    swap = swap_matrix(32, 16)
    for g in range(2):
        block = it_ref[16 * g : 16 * (g + 1)].astype(bf16).reshape(512, CELLS)
        turned = jnp.dot(swap, block, preferred_element_type=f32).astype(bf16)
        rows_ref[:, 16 * g : 16 * (g + 1), :] = turned.reshape(32, 16, CELLS)
    loads[1].wait()
    loads[2].wait()
    blank = jnp.zeros((3, CELLS), f32)
    for side, row in ((0, 0), (1, 31)):
        ce_ref[side] = jnp.concatenate([mean_ref[row : row + 1], kl_ref[:, row, :], blank], 0)
    pl.semaphore_wait(barrier, GROUP + 1)

    def issue(k):
        for peer in peers:
            row = row_of(peer, k)

            def pass_row():
                send(rows_ref.at[row], r_ref.at[k, own_modes], (d, peer), send_sem.at[k], recv_sem.at[k])

            if k > 0:
                pass_row()
            else:
                pl.when((row >= 0) & (row < 32))(pass_row)
        row = row_of(m, k)

        def keep_row():
            pltpu.make_async_copy(rows_ref.at[row], r_ref.at[k, own_modes], recv_sem.at[k]).start()

        if k > 0:
            keep_row()
        else:
            pl.when((row >= 0) & (row < 32))(keep_row)

    def sent(k):
        drain(r_ref.at[k, pl.ds(0, 32 * (GROUP - 1))], send_sem.at[k])

    edges = [
        send(rows_ref.at[31], edge_ref.at[0], (up, m), edge_sem.at[0], edge_sem.at[2]),
        send(rows_ref.at[0], edge_ref.at[1], (down, m), edge_sem.at[1], edge_sem.at[3]),
    ]
    coefs = [
        send(ce_ref.at[1], ch_ref.at[0], (up, m), coef_sem.at[0], coef_sem.at[2]),
        send(ce_ref.at[0], ch_ref.at[1], (down, m), coef_sem.at[1], coef_sem.at[3]),
    ]
    issue(1)
    issue(0)
    loads[3].wait()
    loads[4].wait()
    fill_table(tri_ref, val_ref, table_ref)
    sent(1)
    issue(2)

    for side, holder in ((0, 0), (1, GROUP - 1)):
        edges[side].wait_recv()

        @pl.when(m == holder)
        def _():
            pltpu.make_async_copy(edge_ref.at[side], r_ref.at[0, own_modes], recv_sem.at[0]).start()

        @pl.when(m != holder)
        def _():
            send(edge_ref.at[side], r_ref.at[0, own_modes], (d, holder), send_sem.at[0], recv_sem.at[0])

    fill_mixing(table_ref, mix_ref)
    sent(0)
    issue(3)

    for copy in coefs:
        copy.wait_recv()
    first_edge = jnp.where(d == 0, 0.0, 1.0)
    last_edge = jnp.where(d == count - 1, 0.0, 1.0)
    outer = jnp.where(m == 0, first_edge, jnp.where(m == GROUP - 1, last_edge, 1.0))
    for k in range(6):
        row = row_of(m, k)
        if k == 0:
            row = jnp.minimum(jnp.maximum(row, 0), 31)
        mean_row = mean_ref[pl.ds(row, 1), :]
        kl_row = kl_ref[:, pl.ds(row, 1), :].reshape(NF - 1, CELLS)
        here = jnp.concatenate([mean_row, kl_row, blank], 0)
        if k == 0:
            here = jnp.where(m == 0, ch_ref[0], jnp.where(m == GROUP - 1, ch_ref[1], here)) * outer
        b_ref[k] = 0.5 * here
    place = iota((24, CELLS), 1)
    for k in range(1, 5):
        nb_ref[k - 1] = b_ref[k - 1] + b_ref[k + 1] + lane_neighbours(b_ref[k], place & (NZ - 1), place)

    row = iota((32, CELLS), 0)
    mean = mean_ref[...]
    c0_ref[0] = jnp.where(row == 0, ch_ref[0, 0:1] * first_edge, pltpu.roll(mean, 1, 0))
    c0_ref[1] = mean
    c0_ref[2] = jnp.where(row == 31, ch_ref[1, 0:1] * last_edge, pltpu.roll(mean, 31, 0))
    fill_faces(c0_ref, w_ref, inv_ref)
    near = plane_neighbours()

    def weigh(coef, u, total=None):
        for l in range(NF):
            term = coef[l : l + 1] * u[l]
            total = term if total is None else total + term
        return total

    def mixed(ib, panel):
        return jnp.dot(mix_ref[ib], panel, preferred_element_type=f32).reshape(NF, IB, CELLS)

    def take_plane(k):
        own = s_ref[k]
        high = own.astype(bf16)
        low = (own - high.astype(f32)).astype(bf16)
        around = jnp.dot(high, near, preferred_element_type=f32) + jnp.dot(low, near, preferred_element_type=f32)
        t_ref[k - 1] = t_ref[k - 1] - around

    def mix_slot(k):
        def block(ib, _):
            rows = pl.ds(pl.multiple_of(ib * IB, IB), IB)
            u = mixed(ib, r_ref[k])
            s_ref[k, rows] = weigh(b_ref[k], u)
            if k > 0:
                t_ref[k - 1, rows] = weigh(nb_ref[k - 1], u)
            return 0

        lax.fori_loop(0, NIB, block, 0)
        if k > 0:
            take_plane(k)

    def fill_differences(k):
        own = r_ref[k]
        behind = r_ref[k - 1].astype(f32)
        if k == 1:
            behind = behind * outer
        around = jnp.dot(own, near, preferred_element_type=f32)
        g_ref[...] = (6.0 * own.astype(f32) - around - behind - r_ref[k + 1].astype(f32)).astype(bf16)

    def finish_row(k):
        row = row_of(m, k)

        def block(i, _):
            ib = lax.rem(m + 1 + i, GROUP)
            before = lax.rem(m + i, GROUP)

            @pl.when(i > 0)
            def _():
                modes = pl.ds(pl.multiple_of(before * IB, IB), IB)
                send(out_ref.at[k - 1, modes], img_ref.at[row], (d, before), back_sem.at[k - 1], home_sem.at[k - 1])

            rows = pl.ds(pl.multiple_of(ib * IB, IB), IB)
            u = mixed(ib, r_ref[k + 1])
            following = weigh(b_ref[k + 1], u)
            s_ref[k + 1, rows] = following
            if k < 4:
                t_ref[k, rows] = weigh(nb_ref[k], u)
            v = mixed(ib, g_ref[...])
            total = weigh(b_ref[k], v, t_ref[k - 1, rows] - s_ref[k - 1, rows] - following).astype(bf16)
            out_ref[k - 1, rows] = total

            @pl.when(i == GROUP - 1)
            def _():
                img_ref[row] = total

            return 0

        lax.fori_loop(0, GROUP, block, 0)
        if k < 4:
            take_plane(k + 1)

    seven = pl.ds(0, GROUP - 1)
    drain(r_ref.at[1], recv_sem.at[1])
    mix_slot(1)
    drain(r_ref.at[0], recv_sem.at[0])
    mix_slot(0)
    sent(2)
    issue(4)
    drain(r_ref.at[2], recv_sem.at[2])
    fill_differences(1)
    finish_row(1)
    drain(r_ref.at[3], recv_sem.at[3])
    fill_differences(2)
    finish_row(2)
    drain(r_ref.at[4], recv_sem.at[4])
    forward = send(r_ref.at[4], r_ref.at[5], (d, sibling), send_sem.at[5], recv_sem.at[5])
    fill_differences(3)
    finish_row(3)
    loads[5].wait()
    drain(img_ref.at[seven], home_sem.at[0])
    first_inv = inv_ref[...] * (1.0 / cheb_center)
    for side, row in ((0, 0), (1, 31)):
        fe_ref[side] = (src_ref[:, row, :] - img_ref[row].astype(f32)) * first_inv[row : row + 1]
    forward.wait_recv()
    fill_differences(4)
    firsts = [
        send(fe_ref.at[1], fh_ref.at[0], (up, m), first_sem.at[0], first_sem.at[2]),
        send(fe_ref.at[0], fh_ref.at[1], (down, m), first_sem.at[1], first_sem.at[3]),
    ]
    finish_row(4)

    for copy in firsts:
        copy.wait_recv()
    halo_ref[0] = fh_ref[0] * first_edge
    halo_ref[1] = fh_ref[1] * last_edge
    for copy in edges + coefs + firsts + [forward]:
        copy.wait_send()
    for k in (3, 4):
        sent(k)
    for k in range(1, 4):
        drain(img_ref.at[seven], home_sem.at[k])
    swap = swap_matrix(16, 32)
    for g in range(2):
        block = img_ref[:, 16 * g : 16 * (g + 1), :].reshape(512, CELLS)
        turned = jnp.dot(swap, block, preferred_element_type=f32).astype(bf16)
        nat_ref[16 * g : 16 * (g + 1)] = turned.reshape(16, 32, CELLS)
    for k in range(4):
        drain(out_ref.at[k, pl.ds(0, 32 * (GROUP - 1))], back_sem.at[k])


STEP = 8


def correct_kernel(it_ref, src_ref, nat_ref, halo_ref, w_ref, inv_ref, upd_ref, res_ref):
    row = iota((32, CELLS), 0)

    def update(mode, _):
        res = src_ref[mode] - nat_ref[mode].astype(f32)
        res_ref[mode] = res
        inv = inv_ref[...]
        first = res * inv * (1.0 / cheb_center)
        above = jnp.where(row == 31, halo_ref[1, pl.ds(mode, 1), :], pltpu.roll(first, 31, 0))
        below = jnp.where(row == 0, halo_ref[0, pl.ds(mode, 1), :], pltpu.roll(first, 1, 0))
        around = w_ref[0] * above + w_ref[1] * below
        for f, amount in enumerate((CELLS - NZ, NZ, CELLS - 1, 1)):
            around = around + w_ref[2 + f] * pltpu.roll(first, amount, 1)
        smoothed = res * (1.0 - 1.0 / cheb_center) + around
        second = rho_one * rho_zero * first + (2.0 * rho_one / cheb_radius) * smoothed * inv
        upd_ref[mode] = it_ref[mode] + first + second
        return 0

    lax.fori_loop(0, STEP, update, 0, unroll=2)


def body(iterate, source, mean_coef, kl_fields, tri_index, tri_value):
    sds = jax.ShapeDtypeStruct
    vm = pl.BlockSpec(memory_space=pltpu.VMEM)
    hbm = pl.BlockSpec(memory_space=pltpu.HBM)
    dma = pltpu.SemaphoreType.DMA
    natural, halo, w, inv = pl.pallas_call(
        exchange_kernel,
        out_shape=(
            sds((32, 32, CELLS), bf16),
            sds((2, 32, CELLS), f32),
            sds((6, 32, CELLS), f32),
            sds((32, CELLS), f32),
        ),
        in_specs=[hbm] * 6,
        out_specs=(vm, vm, vm, vm),
        scratch_shapes=[
            pltpu.VMEM((32, 32, CELLS), f32),
            pltpu.VMEM((32, 32, CELLS), f32),
            pltpu.VMEM((32, CELLS), f32),
            pltpu.VMEM((NF - 1, 32, CELLS), f32),
            pltpu.VMEM((3, ENTRIES), i32),
            pltpu.VMEM((42, 128), f32),
            pltpu.VMEM((32, 32, CELLS), bf16),
            pltpu.VMEM((2, 32, CELLS), bf16),
            pltpu.VMEM((6, P_SIZE, CELLS), bf16),
            pltpu.VMEM((NIB, NF * IB, P_SIZE), bf16),
            pltpu.VMEM((P_SIZE, 64), f32),
            pltpu.VMEM((P_SIZE, CELLS), bf16),
            pltpu.VMEM((6, 24, CELLS), f32),
            pltpu.VMEM((4, 24, CELLS), f32),
            pltpu.VMEM((6, P_SIZE, CELLS), f32),
            pltpu.VMEM((4, P_SIZE, CELLS), f32),
            pltpu.VMEM((2, 24, CELLS), f32),
            pltpu.VMEM((2, 24, CELLS), f32),
            pltpu.VMEM((4, P_SIZE, CELLS), bf16),
            pltpu.VMEM((32, 32, CELLS), bf16),
            pltpu.VMEM((2, 32, CELLS), f32),
            pltpu.VMEM((2, 32, CELLS), f32),
            pltpu.VMEM((3, 32, CELLS), f32),
            dma((6,)),
            dma((4,)),
            dma((6,)),
            dma((6,)),
            dma((4,)),
            dma((4,)),
            dma((4,)),
            dma((4,)),
        ],
        compiler_params=pltpu.CompilerParams(
            collective_id=0, has_side_effects=True, vmem_limit_bytes=50 * 2**20
        ),
    )(*[
        pltpu.with_memory_space_constraint(x, pltpu.HBM)
        for x in (iterate, source, mean_coef, kl_fields, tri_index.T, tri_value.reshape(42, 128))
    ])

    big = pl.BlockSpec((STEP, 32, CELLS), lambda g: (g, 0, 0))
    return pl.pallas_call(
        correct_kernel,
        out_shape=(sds((32, 32, CELLS), f32), sds((32, 32, CELLS), f32)),
        grid=(32 // STEP,),
        in_specs=[
            big,
            big,
            big,
            pl.BlockSpec((2, STEP, CELLS), lambda g: (0, g, 0)),
            pl.BlockSpec((6, 32, CELLS), lambda g: (0, 0, 0)),
            pl.BlockSpec((32, CELLS), lambda g: (0, 0)),
        ],
        out_specs=(big, big),
        compiler_params=pltpu.CompilerParams(vmem_limit_bytes=16 * 2**20),
    )(iterate, source, natural, halo, w, inv)


def solution(mesh):
    return jax.shard_map(
        body,
        mesh=mesh,
        in_specs=(
            P("mode", "dom", None),
            P("mode", "dom", None),
            P("dom", None),
            P(None, "dom", None),
            P(),
            P(),
        ),
        out_specs=(P("mode", "dom", None), P("mode", "dom", None)),
        check_vma=False,
    )
```

time: 67.1 us -> 51 us (0.76)
  Pallas kernels: 62.9 us -> 50.3 us
  local copies, waits for them, and re-layouts: 3.37 us -> 0.01 us
    pallas_call x1 -> x2, Pallas kernels: 62.9 us -> 50.3 us  [the longest x1 46.7 us: body(): pl.pallas_call(exchange_kernel, out_shape=(sds((32, 32, CELLS), bf16), sd...]
    unnamed x4, local copies, waits for them, and re-layouts: 3.37 us -> 0.01 us
where the time goes in v3:
time: 51 us; the launch traced here: 50.9 us
  Pallas kernels  50.3 us (99%)
  between operations  0.67 us (1%)
    pallas_call x1, Pallas kernels, body(): pl.pallas_call(exchange_kernel, out_shape=(sds((32, 32, CELLS), bf16), sd...  46.7 us
    pallas_call x1, Pallas kernels, body(): pl.pallas_call(correct_kernel, out_shape=(sds((32, 32, CELLS), f32), sds(...  3.55 us

profile of v3, /device:TPU:1, one launch (start us, length us, event | category | flops | bytes accessed | tf_op | source)
XLA Modules:
  0.0 50.9 jit_solution(8572613371814217380)
XLA Ops:
  0.6 0.0 copy-start
  0.6 0.0 copy-start.1
  0.7 46.7 %shard_map.77 = (bf16[32,32,256]{2,1,0:T(8,128)(2,1)S(1)}, f32[2,32,256]{2,1,0:T(8,128)S(1)}, f32[6,32,256]{2,1,0:T(8,128)S(1)}, f32[32,256]{1,0:T(8,128)S(1)}) custom-call(f32[32,32,256]{2,1,0:T(8,128)} %it_ref.1, f32[32,32,256]{2,1,0:T(8,128)} %src_ref.1, f32[32,256]{1,0:T(8,128)} %mean_hbm.1, f32[20,32,256]{2,1,0:T(8,128)} %kl_hbm.1, s32[3,5376]{1,0:T(4,128)} %bitcast.2, ...), custom_call_target="tpu_custom_call" | custom-call | tf_op jit(solution)/shard_map/pallas_call | solution.py:396
  47.4 0.0 copy-done
  47.4 0.0 copy-done.1
  47.4 3.5 %shard_map.78 = (f32[32,32,256]{2,1,0:T(8,128)}, f32[32,32,256]{2,1,0:T(8,128)}) custom-call(f32[32,32,256]{2,1,0:T(8,128)S(1)} %copy-done, f32[32,32,256]{2,1,0:T(8,128)S(1)} %copy-done.1, bf16[32,32,256]{2,1,0:T(8,128)(2,1)S(1)} %get-tuple-element.6.nat_ref, f32[2,32,256]{2,1,0:T(8,128)S(1)} %get-tuple-element.7.halo_ref, ...), custom_call_target="tpu_custom_call" | custom-call | tf_op jit(solution)/shard_map/pallas_call | solution.py:448
Async XLA Ops:
  0.6 46.7 %copy-start = (f32[32,32,256]{2,1,0:T(8,128)S(1)}, f32[32,32,256]{2,1,0:T(8,128)}, u32[]{:S(2)}) copy-start(f32[32,32,256]{2,1,0:T(8,128)} %it_ref.1) | copy-start | bytes 3145732
  0.6 46.7 %copy-start.1 = (f32[32,32,256]{2,1,0:T(8,128)S(1)}, f32[32,32,256]{2,1,0:T(8,128)}, u32[]{:S(2)}) copy-start(f32[32,32,256]{2,1,0:T(8,128)} %src_ref.1) | copy-start | bytes 3145732

commit v4 on v3

--- a/solution.py
+++ b/solution.py
@@ -107,9 +107,9 @@
 
 def exchange_kernel(
     it_hbm, src_hbm, mean_hbm, kl_hbm, tri_hbm, val_hbm, nat_ref, halo_ref, w_ref, inv_ref,
-    it_ref, src_ref, mean_ref, kl_ref, tri_ref, val_ref, rows_ref, edge_ref, r_ref, mix_ref, table_ref, g_ref, b_ref, nb_ref, s_ref, t_ref,
+    it_ref, src_ref, mean_ref, kl_ref, tri_ref, val_ref, rows_ref, pair_ref, edge_ref, r_ref, mix_ref, table_ref, g_ref, b_ref, nb_ref, s_ref, t_ref,
     ce_ref, ch_ref, out_ref, img_ref, fe_ref, fh_ref, c0_ref,
-    local_sem, edge_sem, send_sem, recv_sem, coef_sem, back_sem, home_sem, first_sem,
+    local_sem, edge_sem, send_sem, recv_sem, coef_sem, back_sem, home_sem, first_sem, pair_sem, go_sem,
 ):
     d = lax.axis_index("dom")
     m = lax.axis_index("mode")
@@ -145,11 +145,19 @@
     ]
     for load in loads:
         load.start()
+    even = lax.rem(m, 2) == 0
+    odd = lax.rem(m, 2) == 1
     barrier = pltpu.get_barrier_semaphore()
     for peer in peers:
-        pl.semaphore_signal(barrier, inc=1, device_id=(d, peer), device_id_type=MESH)
-    for other in (up, down):
-        pl.semaphore_signal(barrier, inc=1, device_id=(other, m), device_id_type=MESH)
+
+        @pl.when(lax.rem(peer, 2) == 0)
+        def _():
+            pl.semaphore_signal(barrier, inc=1, device_id=(d, peer), device_id_type=MESH)
+
+    @pl.when(odd)
+    def _():
+        for other in (up, down):
+            pl.semaphore_signal(barrier, inc=1, device_id=(other, m), device_id_type=MESH)
 
     loads[0].wait()
     swap = swap_matrix(32, 16)
@@ -157,12 +165,22 @@
         block = it_ref[16 * g : 16 * (g + 1)].astype(bf16).reshape(512, CELLS)
         turned = jnp.dot(swap, block, preferred_element_type=f32).astype(bf16)
         rows_ref[:, 16 * g : 16 * (g + 1), :] = turned.reshape(32, 16, CELLS)
+    pair_ref[0, 32:64] = rows_ref[0]
+    pair_ref[1, 32:64] = rows_ref[31]
     loads[1].wait()
     loads[2].wait()
     blank = jnp.zeros((3, CELLS), f32)
     for side, row in ((0, 0), (1, 31)):
         ce_ref[side] = jnp.concatenate([mean_ref[row : row + 1], kl_ref[:, row, :], blank], 0)
-    pl.semaphore_wait(barrier, GROUP + 1)
+
+    @pl.when(even)
+    def _():
+        pl.semaphore_wait(barrier, GROUP - 1)
+        pl.semaphore_signal(go_sem, inc=1, device_id=(d, sibling), device_id_type=MESH)
+
+    @pl.when(odd)
+    def _():
+        pl.semaphore_wait(go_sem, 1)
 
     def issue(k):
         for peer in peers:
@@ -188,55 +206,167 @@
     def sent(k):
         drain(r_ref.at[k, pl.ds(0, 32 * (GROUP - 1))], send_sem.at[k])
 
-    edges = [
-        send(rows_ref.at[31], edge_ref.at[0], (up, m), edge_sem.at[0], edge_sem.at[2]),
-        send(rows_ref.at[0], edge_ref.at[1], (down, m), edge_sem.at[1], edge_sem.at[3]),
-    ]
-    coefs = [
-        send(ce_ref.at[1], ch_ref.at[0], (up, m), coef_sem.at[0], coef_sem.at[2]),
-        send(ce_ref.at[0], ch_ref.at[1], (down, m), coef_sem.at[1], coef_sem.at[3]),
-    ]
+    @pl.when(even)
+    def _():
+        for side, row in ((0, 0), (1, 31)):
+            send(rows_ref.at[row], pair_ref.at[side, pl.ds(0, 32)], (d, sibling), pair_sem.at[side], pair_sem.at[2 + side])
+
     issue(1)
-    issue(0)
+    issue(2)
     loads[3].wait()
     loads[4].wait()
     fill_table(tri_ref, val_ref, table_ref)
     sent(1)
-    issue(2)
-
-    for side, holder in ((0, 0), (1, GROUP - 1)):
-        edges[side].wait_recv()
-
-        @pl.when(m == holder)
-        def _():
-            pltpu.make_async_copy(edge_ref.at[side], r_ref.at[0, own_modes], recv_sem.at[0]).start()
-
-        @pl.when(m != holder)
-        def _():
-            send(edge_ref.at[side], r_ref.at[0, own_modes], (d, holder), send_sem.at[0], recv_sem.at[0])
-
+    issue(3)
     fill_mixing(table_ref, mix_ref)
-    sent(0)
-    issue(3)
-
-    for copy in coefs:
-        copy.wait_recv()
+
     first_edge = jnp.where(d == 0, 0.0, 1.0)
     last_edge = jnp.where(d == count - 1, 0.0, 1.0)
     outer = jnp.where(m == 0, first_edge, jnp.where(m == GROUP - 1, last_edge, 1.0))
-    for k in range(6):
-        row = row_of(m, k)
-        if k == 0:
-            row = jnp.minimum(jnp.maximum(row, 0), 31)
-        mean_row = mean_ref[pl.ds(row, 1), :]
+
+    def coef_row(row):
         kl_row = kl_ref[:, pl.ds(row, 1), :].reshape(NF - 1, CELLS)
-        here = jnp.concatenate([mean_row, kl_row, blank], 0)
-        if k == 0:
-            here = jnp.where(m == 0, ch_ref[0], jnp.where(m == GROUP - 1, ch_ref[1], here)) * outer
-        b_ref[k] = 0.5 * here
+        return jnp.concatenate([mean_ref[pl.ds(row, 1), :], kl_row, blank], 0)
+
+    for k in range(1, 6):
+        b_ref[k] = 0.5 * coef_row(row_of(m, k))
     place = iota((24, CELLS), 1)
     for k in range(1, 5):
-        nb_ref[k - 1] = b_ref[k - 1] + b_ref[k + 1] + lane_neighbours(b_ref[k], place & (NZ - 1), place)
+        beside = b_ref[k + 1] if k == 1 else b_ref[k - 1] + b_ref[k + 1]
+        nb_ref[k - 1] = beside + lane_neighbours(b_ref[k], place & (NZ - 1), place)
+    near = plane_neighbours()
+    sent(2)
+    issue(4)
+
+    def weigh(coef, u, total=None):
+        for l in range(NF):
+            term = coef[l : l + 1] * u[l]
+            total = term if total is None else total + term
+        return total
+
+    def mixed(ib, panel):
+        return jnp.dot(mix_ref[ib], panel, preferred_element_type=f32).reshape(NF, IB, CELLS)
+
+    def take_plane(k):
+        own = s_ref[k]
+        high = own.astype(bf16)
+        low = (own - high.astype(f32)).astype(bf16)
+        around = jnp.dot(high, near, preferred_element_type=f32) + jnp.dot(low, near, preferred_element_type=f32)
+        t_ref[k - 1] = t_ref[k - 1] - around
+
+    def mix_slot(k):
+        def block(ib, _):
+            rows = pl.ds(pl.multiple_of(ib * IB, IB), IB)
+            u = mixed(ib, r_ref[k])
+            s_ref[k, rows] = weigh(b_ref[k], u)
+            t_ref[k - 1, rows] = weigh(nb_ref[k - 1], u)
+            return 0
+
+        lax.fori_loop(0, NIB, block, 0)
+        take_plane(k)
+
+    def fill_differences(k):
+        own = r_ref[k]
+        behind = r_ref[k - 1].astype(f32)
+        if k == 1:
+            behind = behind * outer
+            r_ref[0] = (own.astype(f32) - behind).astype(bf16)
+        around = jnp.dot(own, near, preferred_element_type=f32)
+        g_ref[...] = (6.0 * own.astype(f32) - around - behind - r_ref[k + 1].astype(f32)).astype(bf16)
+
+    def finish_row(k):
+        row = row_of(m, k)
+        beside = 0 if k == 1 else k + 1
+        other = 2 if k == 1 else k - 1
+
+        def block(i, _):
+            ib = lax.rem(m + 1 + i, GROUP)
+            before = lax.rem(m + i, GROUP)
+
+            @pl.when(i > 0)
+            def _():
+                modes = pl.ds(pl.multiple_of(before * IB, IB), IB)
+                send(out_ref.at[k - 1, modes], img_ref.at[row], (d, before), back_sem.at[k - 1], home_sem.at[k - 1])
+
+            rows = pl.ds(pl.multiple_of(ib * IB, IB), IB)
+            u = mixed(ib, r_ref[beside])
+            sums = weigh(b_ref[beside], u)
+            if beside in (3, 4):
+                s_ref[beside, rows] = sums
+                t_ref[beside - 1, rows] = weigh(nb_ref[beside - 1], u)
+            v = mixed(ib, g_ref[...])
+            start = t_ref[k - 1, rows] - s_ref[other, rows]
+            start = start + sums if k == 1 else start - sums
+            total = weigh(b_ref[k], v, start).astype(bf16)
+            out_ref[k - 1, rows] = total
+
+            @pl.when(i == GROUP - 1)
+            def _():
+                img_ref[row] = total
+
+            return 0
+
+        lax.fori_loop(0, GROUP, block, 0)
+        if beside in (3, 4):
+            take_plane(beside)
+
+    seven = pl.ds(0, GROUP - 1)
+    drain(r_ref.at[1], recv_sem.at[1])
+    mix_slot(1)
+
+    @pl.when(odd)
+    def _():
+        pl.semaphore_wait(barrier, 2)
+        for side in range(2):
+            drain(pair_ref.at[side, pl.ds(0, 32)], pair_sem.at[2 + side])
+        send(pair_ref.at[1], edge_ref.at[0], (up, m), edge_sem.at[0], edge_sem.at[2])
+        send(pair_ref.at[0], edge_ref.at[1], (down, m), edge_sem.at[1], edge_sem.at[3])
+        send(ce_ref.at[1], ch_ref.at[0], (up, m), coef_sem.at[0], coef_sem.at[2])
+        send(ce_ref.at[0], ch_ref.at[1], (down, m), coef_sem.at[1], coef_sem.at[3])
+
+    drain(r_ref.at[2], recv_sem.at[2])
+    mix_slot(2)
+    sent(3)
+    issue(0)
+    drain(r_ref.at[3], recv_sem.at[3])
+    fill_differences(2)
+    finish_row(2)
+
+    both_modes = pl.ds(pl.multiple_of((m // 2) * 64, 64), 64)
+
+    @pl.when(odd)
+    def _():
+        for side, holder in ((0, 0), (1, GROUP - 1)):
+            drain(edge_ref.at[side], edge_sem.at[2 + side])
+
+            @pl.when(m == holder)
+            def _():
+                pltpu.make_async_copy(edge_ref.at[side], r_ref.at[0, both_modes], recv_sem.at[0]).start()
+
+            @pl.when(m != holder)
+            def _():
+                send(edge_ref.at[side], r_ref.at[0, both_modes], (d, holder), pair_sem.at[4 + side], recv_sem.at[0])
+
+        for side in range(2):
+            drain(ch_ref.at[side], coef_sem.at[2 + side])
+        send(ch_ref, ch_ref, (d, sibling), coef_sem.at[4], coef_sem.at[5])
+
+    drain(r_ref.at[4], recv_sem.at[4])
+    forward = send(r_ref.at[4], r_ref.at[5], (d, sibling), send_sem.at[5], recv_sem.at[5])
+    fill_differences(3)
+    finish_row(3)
+
+    @pl.when(even)
+    def _():
+        drain(ch_ref, coef_sem.at[5])
+
+    row = row_of(m, 0)
+    inside = coef_row(jnp.minimum(jnp.maximum(row, 0), 31))
+    edge_coef = jnp.where(m == 0, ch_ref[0], jnp.where(m == GROUP - 1, ch_ref[1], inside))
+    b_ref[0] = 0.5 * outer * edge_coef
+    drain(r_ref.at[0], recv_sem.at[0])
+    fill_differences(1)
+    finish_row(1)
 
     row = iota((32, CELLS), 0)
     mean = mean_ref[...]
@@ -244,124 +374,63 @@
     c0_ref[1] = mean
     c0_ref[2] = jnp.where(row == 31, ch_ref[1, 0:1] * last_edge, pltpu.roll(mean, 31, 0))
     fill_faces(c0_ref, w_ref, inv_ref)
-    near = plane_neighbours()
-
-    def weigh(coef, u, total=None):
-        for l in range(NF):
-            term = coef[l : l + 1] * u[l]
-            total = term if total is None else total + term
-        return total
-
-    def mixed(ib, panel):
-        return jnp.dot(mix_ref[ib], panel, preferred_element_type=f32).reshape(NF, IB, CELLS)
-
-    def take_plane(k):
-        own = s_ref[k]
-        high = own.astype(bf16)
-        low = (own - high.astype(f32)).astype(bf16)
-        around = jnp.dot(high, near, preferred_element_type=f32) + jnp.dot(low, near, preferred_element_type=f32)
-        t_ref[k - 1] = t_ref[k - 1] - around
-
-    def mix_slot(k):
-        def block(ib, _):
-            rows = pl.ds(pl.multiple_of(ib * IB, IB), IB)
-            u = mixed(ib, r_ref[k])
-            s_ref[k, rows] = weigh(b_ref[k], u)
-            if k > 0:
-                t_ref[k - 1, rows] = weigh(nb_ref[k - 1], u)
-            return 0
-
-        lax.fori_loop(0, NIB, block, 0)
-        if k > 0:
-            take_plane(k)
-
-    def fill_differences(k):
-        own = r_ref[k]
-        behind = r_ref[k - 1].astype(f32)
-        if k == 1:
-            behind = behind * outer
-        around = jnp.dot(own, near, preferred_element_type=f32)
-        g_ref[...] = (6.0 * own.astype(f32) - around - behind - r_ref[k + 1].astype(f32)).astype(bf16)
-
-    def finish_row(k):
-        row = row_of(m, k)
-
-        def block(i, _):
-            ib = lax.rem(m + 1 + i, GROUP)
-            before = lax.rem(m + i, GROUP)
-
-            @pl.when(i > 0)
-            def _():
-                modes = pl.ds(pl.multiple_of(before * IB, IB), IB)
-                send(out_ref.at[k - 1, modes], img_ref.at[row], (d, before), back_sem.at[k - 1], home_sem.at[k - 1])
-
-            rows = pl.ds(pl.multiple_of(ib * IB, IB), IB)
-            u = mixed(ib, r_ref[k + 1])
-            following = weigh(b_ref[k + 1], u)
-            s_ref[k + 1, rows] = following
-            if k < 4:
-                t_ref[k, rows] = weigh(nb_ref[k], u)
-            v = mixed(ib, g_ref[...])
-            total = weigh(b_ref[k], v, t_ref[k - 1, rows] - s_ref[k - 1, rows] - following).astype(bf16)
-            out_ref[k - 1, rows] = total
-
-            @pl.when(i == GROUP - 1)
-            def _():
-                img_ref[row] = total
-
-            return 0
-
-        lax.fori_loop(0, GROUP, block, 0)
-        if k < 4:
-            take_plane(k + 1)
-
-    seven = pl.ds(0, GROUP - 1)
-    drain(r_ref.at[1], recv_sem.at[1])
-    mix_slot(1)
-    drain(r_ref.at[0], recv_sem.at[0])
-    mix_slot(0)
-    sent(2)
-    issue(4)
-    drain(r_ref.at[2], recv_sem.at[2])
-    fill_differences(1)
-    finish_row(1)
-    drain(r_ref.at[3], recv_sem.at[3])
-    fill_differences(2)
-    finish_row(2)
-    drain(r_ref.at[4], recv_sem.at[4])
-    forward = send(r_ref.at[4], r_ref.at[5], (d, sibling), send_sem.at[5], recv_sem.at[5])
-    fill_differences(3)
-    finish_row(3)
+    forward.wait_recv()
+    fill_differences(4)
+    finish_row(4)
+
     loads[5].wait()
     drain(img_ref.at[seven], home_sem.at[0])
     first_inv = inv_ref[...] * (1.0 / cheb_center)
     for side, row in ((0, 0), (1, 31)):
         fe_ref[side] = (src_ref[:, row, :] - img_ref[row].astype(f32)) * first_inv[row : row + 1]
-    forward.wait_recv()
-    fill_differences(4)
+    swap = swap_matrix(16, 32)
     firsts = [
         send(fe_ref.at[1], fh_ref.at[0], (up, m), first_sem.at[0], first_sem.at[2]),
         send(fe_ref.at[0], fh_ref.at[1], (down, m), first_sem.at[1], first_sem.at[3]),
     ]
-    finish_row(4)
-
-    for copy in firsts:
-        copy.wait_recv()
-    halo_ref[0] = fh_ref[0] * first_edge
-    halo_ref[1] = fh_ref[1] * last_edge
-    for copy in edges + coefs + firsts + [forward]:
-        copy.wait_send()
-    for k in (3, 4):
-        sent(k)
     for k in range(1, 4):
         drain(img_ref.at[seven], home_sem.at[k])
-    swap = swap_matrix(16, 32)
     for g in range(2):
         block = img_ref[:, 16 * g : 16 * (g + 1), :].reshape(512, CELLS)
         turned = jnp.dot(swap, block, preferred_element_type=f32).astype(bf16)
         nat_ref[16 * g : 16 * (g + 1)] = turned.reshape(16, 32, CELLS)
+
+    @pl.when(odd)
+    def _():
+        for side, holder in ((0, 0), (1, GROUP - 1)):
+            drain(edge_ref.at[side], edge_sem.at[side])
+            drain(ce_ref.at[side], coef_sem.at[side])
+
+            @pl.when(m != holder)
+            def _():
+                drain(edge_ref.at[side], pair_sem.at[4 + side])
+
+        drain(ch_ref, coef_sem.at[4])
+
+    @pl.when(even)
+    def _():
+        for side in range(2):
+            drain(pair_ref.at[side, pl.ds(0, 32)], pair_sem.at[side])
+
+    outermost = (m == 0) | (m == GROUP - 1)
+
+    @pl.when(outermost)
+    def _():
+        drain(r_ref.at[1, pl.ds(0, 32 * (GROUP - 2))], send_sem.at[0])
+
+    @pl.when(jnp.logical_not(outermost))
+    def _():
+        drain(r_ref.at[1, pl.ds(0, 32 * (GROUP - 3))], send_sem.at[0])
+
+    sent(4)
+    forward.wait_send()
     for k in range(4):
         drain(out_ref.at[k, pl.ds(0, 32 * (GROUP - 1))], back_sem.at[k])
+    for copy in firsts:
+        copy.wait_send()
+        copy.wait_recv()
+    halo_ref[0] = fh_ref[0] * first_edge
+    halo_ref[1] = fh_ref[1] * last_edge
 
 
 STEP = 8
@@ -411,7 +480,8 @@
             pltpu.VMEM((3, ENTRIES), i32),
             pltpu.VMEM((42, 128), f32),
             pltpu.VMEM((32, 32, CELLS), bf16),
-            pltpu.VMEM((2, 32, CELLS), bf16),
+            pltpu.VMEM((2, 64, CELLS), bf16),
+            pltpu.VMEM((2, 64, CELLS), bf16),
             pltpu.VMEM((6, P_SIZE, CELLS), bf16),
             pltpu.VMEM((NIB, NF * IB, P_SIZE), bf16),
             pltpu.VMEM((P_SIZE, 64), f32),
@@ -431,10 +501,12 @@
             dma((4,)),
             dma((6,)),
             dma((6,)),
+            dma((6,)),
             dma((4,)),
             dma((4,)),
             dma((4,)),
-            dma((4,)),
+            dma((6,)),
+            pltpu.SemaphoreType.REGULAR,
         ],
         compiler_params=pltpu.CompilerParams(
             collective_id=0, has_side_effects=True, vmem_limit_bytes=50 * 2**20

time: 51 us -> 48.8 us (0.957)
  Pallas kernels: 50.3 us -> 48.1 us
    pallas_call x1, Pallas kernels: 46.7 us -> 44.5 us  [body(): pl.pallas_call(exchange_kernel, out_shape=(sds((32, 32, CELLS), bf16), sd...]
where the time goes in v4:
time: 48.8 us
  Pallas kernels  48.1 us (99%)
  between operations  0.67 us (1%)
    pallas_call x1, Pallas kernels, body(): pl.pallas_call(exchange_kernel, out_shape=(sds((32, 32, CELLS), bf16), sd...  44.5 us
    pallas_call x1, Pallas kernels, body(): pl.pallas_call(correct_kernel, out_shape=(sds((32, 32, CELLS), f32), sds(...  3.55 us

profile of v4, /device:TPU:1, one launch (start us, length us, event | category | flops | bytes accessed | tf_op | source)
XLA Modules:
  0.0 48.8 jit_solution(13220725905238966519)
XLA Ops:
  0.6 0.0 copy-start
  0.6 0.0 copy-start.1
  0.7 44.5 %shard_map.77 = (bf16[32,32,256]{2,1,0:T(8,128)(2,1)S(1)}, f32[2,32,256]{2,1,0:T(8,128)S(1)}, f32[6,32,256]{2,1,0:T(8,128)S(1)}, f32[32,256]{1,0:T(8,128)S(1)}) custom-call(f32[32,32,256]{2,1,0:T(8,128)} %it_ref.1, f32[32,32,256]{2,1,0:T(8,128)} %src_ref.1, f32[32,256]{1,0:T(8,128)} %mean_hbm.1, f32[20,32,256]{2,1,0:T(8,128)} %kl_hbm.1, s32[3,5376]{1,0:T(4,128)} %bitcast.2, ...), custom_call_target="tpu_custom_call" | custom-call | tf_op jit(solution)/shard_map/pallas_call | solution.py:465
  45.2 0.0 copy-done
  45.2 0.0 copy-done.1
  45.2 3.5 %shard_map.78 = (f32[32,32,256]{2,1,0:T(8,128)}, f32[32,32,256]{2,1,0:T(8,128)}) custom-call(f32[32,32,256]{2,1,0:T(8,128)S(1)} %copy-done, f32[32,32,256]{2,1,0:T(8,128)S(1)} %copy-done.1, bf16[32,32,256]{2,1,0:T(8,128)(2,1)S(1)} %get-tuple-element.6.nat_ref, f32[2,32,256]{2,1,0:T(8,128)S(1)} %get-tuple-element.7.halo_ref, ...), custom_call_target="tpu_custom_call" | custom-call | tf_op jit(solution)/shard_map/pallas_call | solution.py:520
Async XLA Ops:
  0.6 44.6 %copy-start = (f32[32,32,256]{2,1,0:T(8,128)S(1)}, f32[32,32,256]{2,1,0:T(8,128)}, u32[]{:S(2)}) copy-start(f32[32,32,256]{2,1,0:T(8,128)} %it_ref.1) | copy-start | bytes 3145732
  0.6 44.6 %copy-start.1 = (f32[32,32,256]{2,1,0:T(8,128)S(1)}, f32[32,32,256]{2,1,0:T(8,128)}, u32[]{:S(2)}) copy-start(f32[32,32,256]{2,1,0:T(8,128)} %src_ref.1) | copy-start | bytes 3145732

commit v5 on v4

--- a/solution.py
+++ b/solution.py
@@ -9,8 +9,10 @@
 NF = 21
 NZ = 16
 CELLS = 256
-IB = 32
+IB = 64
 NIB = P_SIZE // IB
+SUB = 16
+PER = IB // 32
 ENTRIES = P_SIZE * NF
 
 cheb_center = 1.125
@@ -93,7 +95,12 @@
         w = 0.5 * (c + jnp.where(inside, pltpu.roll(c, amount, 1), 0.0))
         diag = diag + w
         w_ref[2 + f] = jnp.where(inside, w, 0.0)
-    inv_ref[...] = 1.0 / diag
+    inv = 1.0 / diag
+    weight = (2.0 * rho_one / cheb_radius) * inv
+    for f in range(6):
+        w_ref[f] = w_ref[f] * weight
+    inv_ref[0] = inv * (1.0 / cheb_center)
+    inv_ref[1] = inv * ((1.0 + rho_one * rho_zero) / cheb_center) + weight * (1.0 - 1.0 / cheb_center)
 
 
 MESH = pl.DeviceIdType.MESH
@@ -107,7 +114,7 @@
 
 def exchange_kernel(
     it_hbm, src_hbm, mean_hbm, kl_hbm, tri_hbm, val_hbm, nat_ref, halo_ref, w_ref, inv_ref,
-    it_ref, src_ref, mean_ref, kl_ref, tri_ref, val_ref, rows_ref, pair_ref, edge_ref, r_ref, mix_ref, table_ref, g_ref, b_ref, nb_ref, s_ref, t_ref,
+    it_ref, src_ref, mean_ref, kl_ref, tri_ref, val_ref, rows_ref, pair_ref, edge_ref, r_ref, mix_ref, table_ref, g_ref, b_ref, nb_ref, s_ref, t_ref, u_ref, v_ref,
     ce_ref, ch_ref, out_ref, img_ref, fe_ref, fh_ref, c0_ref,
     local_sem, edge_sem, send_sem, recv_sem, coef_sem, back_sem, home_sem, first_sem, pair_sem, go_sem,
 ):
@@ -238,14 +245,17 @@
     sent(2)
     issue(4)
 
-    def weigh(coef, u, total=None):
+    def mixed(ib, panel, into):
+        into[...] = jnp.dot(mix_ref[ib], panel, preferred_element_type=f32)
+
+    def weigh(pairs, source, q, totals):
+        totals = list(totals)
         for l in range(NF):
-            term = coef[l : l + 1] * u[l]
-            total = term if total is None else total + term
-        return total
-
-    def mixed(ib, panel):
-        return jnp.dot(mix_ref[ib], panel, preferred_element_type=f32).reshape(NF, IB, CELLS)
+            piece = source[l * IB + q : l * IB + q + SUB]
+            for n, coef in enumerate(pairs):
+                term = coef[l : l + 1] * piece
+                totals[n] = term if totals[n] is None else totals[n] + term
+        return totals
 
     def take_plane(k):
         own = s_ref[k]
@@ -256,10 +266,10 @@
 
     def mix_slot(k):
         def block(ib, _):
-            rows = pl.ds(pl.multiple_of(ib * IB, IB), IB)
-            u = mixed(ib, r_ref[k])
-            s_ref[k, rows] = weigh(b_ref[k], u)
-            t_ref[k - 1, rows] = weigh(nb_ref[k - 1], u)
+            mixed(ib, r_ref[k], u_ref)
+            for q in range(0, IB, SUB):
+                here = pl.ds(pl.multiple_of(ib * IB + q, SUB), SUB)
+                s_ref[k, here], t_ref[k - 1, here] = weigh((b_ref.at[k], nb_ref.at[k - 1]), u_ref, q, (None, None))
             return 0
 
         lax.fori_loop(0, NIB, block, 0)
@@ -279,36 +289,45 @@
         beside = 0 if k == 1 else k + 1
         other = 2 if k == 1 else k - 1
 
+        def pass_on(device):
+            modes = pl.ds(pl.multiple_of(device * 32, 32), 32)
+            send(out_ref.at[k - 1, modes], img_ref.at[row], (d, device), back_sem.at[k - 1], home_sem.at[k - 1])
+
         def block(i, _):
-            ib = lax.rem(m + 1 + i, GROUP)
-            before = lax.rem(m + i, GROUP)
+            ib = lax.rem(m // PER + 1 + i, NIB)
+            before = lax.rem(m // PER + i, NIB)
 
             @pl.when(i > 0)
             def _():
-                modes = pl.ds(pl.multiple_of(before * IB, IB), IB)
-                send(out_ref.at[k - 1, modes], img_ref.at[row], (d, before), back_sem.at[k - 1], home_sem.at[k - 1])
-
-            rows = pl.ds(pl.multiple_of(ib * IB, IB), IB)
-            u = mixed(ib, r_ref[beside])
-            sums = weigh(b_ref[beside], u)
-            if beside in (3, 4):
-                s_ref[beside, rows] = sums
-                t_ref[beside - 1, rows] = weigh(nb_ref[beside - 1], u)
-            v = mixed(ib, g_ref[...])
-            start = t_ref[k - 1, rows] - s_ref[other, rows]
-            start = start + sums if k == 1 else start - sums
-            total = weigh(b_ref[k], v, start).astype(bf16)
-            out_ref[k - 1, rows] = total
-
-            @pl.when(i == GROUP - 1)
-            def _():
-                img_ref[row] = total
-
+                for q in range(PER):
+                    pass_on(PER * before + q)
+
+            mixed(ib, r_ref[beside], u_ref)
+            mixed(ib, g_ref[...], v_ref)
+            for q in range(0, IB, SUB):
+                here = pl.ds(pl.multiple_of(ib * IB + q, SUB), SUB)
+                start = t_ref[k - 1, here] - s_ref[other, here]
+                if beside in (3, 4):
+                    sums, extra = weigh((b_ref.at[beside], nb_ref.at[beside - 1]), u_ref, q, (None, None))
+                    s_ref[beside, here] = sums
+                    t_ref[beside - 1, here] = extra
+                else:
+                    (sums,) = weigh((b_ref.at[beside],), u_ref, q, (None,))
+                start = start + sums if k == 1 else start - sums
+                (total,) = weigh((b_ref.at[k],), v_ref, q, (start,))
+                out_ref[k - 1, here] = total.astype(bf16)
             return 0
 
-        lax.fori_loop(0, GROUP, block, 0)
+        lax.fori_loop(0, NIB, block, 0)
         if beside in (3, 4):
             take_plane(beside)
+        img_ref[row] = out_ref[k - 1, own_modes]
+
+        def rest():
+            for q in range(1, PER):
+                pass_on(PER * (m // PER) + lax.rem(m + q, PER))
+
+        return rest
 
     seven = pl.ds(0, GROUP - 1)
     drain(r_ref.at[1], recv_sem.at[1])
@@ -330,7 +349,7 @@
     issue(0)
     drain(r_ref.at[3], recv_sem.at[3])
     fill_differences(2)
-    finish_row(2)
+    finish_row(2)()
 
     both_modes = pl.ds(pl.multiple_of((m // 2) * 64, 64), 64)
 
@@ -354,7 +373,7 @@
     drain(r_ref.at[4], recv_sem.at[4])
     forward = send(r_ref.at[4], r_ref.at[5], (d, sibling), send_sem.at[5], recv_sem.at[5])
     fill_differences(3)
-    finish_row(3)
+    finish_row(3)()
 
     @pl.when(even)
     def _():
@@ -366,7 +385,7 @@
     b_ref[0] = 0.5 * outer * edge_coef
     drain(r_ref.at[0], recv_sem.at[0])
     fill_differences(1)
-    finish_row(1)
+    last = finish_row(1)
 
     row = iota((32, CELLS), 0)
     mean = mean_ref[...]
@@ -374,13 +393,14 @@
     c0_ref[1] = mean
     c0_ref[2] = jnp.where(row == 31, ch_ref[1, 0:1] * last_edge, pltpu.roll(mean, 31, 0))
     fill_faces(c0_ref, w_ref, inv_ref)
+    last()
     forward.wait_recv()
     fill_differences(4)
-    finish_row(4)
-
+    last = finish_row(4)
     loads[5].wait()
+    last()
     drain(img_ref.at[seven], home_sem.at[0])
-    first_inv = inv_ref[...] * (1.0 / cheb_center)
+    first_inv = inv_ref[0]
     for side, row in ((0, 0), (1, 31)):
         fe_ref[side] = (src_ref[:, row, :] - img_ref[row].astype(f32)) * first_inv[row : row + 1]
     swap = swap_matrix(16, 32)
@@ -442,19 +462,16 @@
     def update(mode, _):
         res = src_ref[mode] - nat_ref[mode].astype(f32)
         res_ref[mode] = res
-        inv = inv_ref[...]
-        first = res * inv * (1.0 / cheb_center)
+        first = res * inv_ref[0]
+        total = it_ref[mode] + res * inv_ref[1]
+        for f, amount in enumerate((CELLS - NZ, NZ, CELLS - 1, 1)):
+            total = total + w_ref[2 + f] * pltpu.roll(first, amount, 1)
         above = jnp.where(row == 31, halo_ref[1, pl.ds(mode, 1), :], pltpu.roll(first, 31, 0))
         below = jnp.where(row == 0, halo_ref[0, pl.ds(mode, 1), :], pltpu.roll(first, 1, 0))
-        around = w_ref[0] * above + w_ref[1] * below
-        for f, amount in enumerate((CELLS - NZ, NZ, CELLS - 1, 1)):
-            around = around + w_ref[2 + f] * pltpu.roll(first, amount, 1)
-        smoothed = res * (1.0 - 1.0 / cheb_center) + around
-        second = rho_one * rho_zero * first + (2.0 * rho_one / cheb_radius) * smoothed * inv
-        upd_ref[mode] = it_ref[mode] + first + second
+        upd_ref[mode] = total + w_ref[0] * above + w_ref[1] * below
         return 0
 
-    lax.fori_loop(0, STEP, update, 0, unroll=2)
+    lax.fori_loop(0, STEP, update, 0, unroll=4)
 
 
 def body(iterate, source, mean_coef, kl_fields, tri_index, tri_value):
@@ -468,7 +485,7 @@
             sds((32, 32, CELLS), bf16),
             sds((2, 32, CELLS), f32),
             sds((6, 32, CELLS), f32),
-            sds((32, CELLS), f32),
+            sds((2, 32, CELLS), f32),
         ),
         in_specs=[hbm] * 6,
         out_specs=(vm, vm, vm, vm),
@@ -490,6 +507,8 @@
             pltpu.VMEM((4, 24, CELLS), f32),
             pltpu.VMEM((6, P_SIZE, CELLS), f32),
             pltpu.VMEM((4, P_SIZE, CELLS), f32),
+            pltpu.VMEM((NF * IB, CELLS), f32),
+            pltpu.VMEM((NF * IB, CELLS), f32),
             pltpu.VMEM((2, 24, CELLS), f32),
             pltpu.VMEM((2, 24, CELLS), f32),
             pltpu.VMEM((4, P_SIZE, CELLS), bf16),
@@ -527,7 +546,7 @@
             big,
             pl.BlockSpec((2, STEP, CELLS), lambda g: (0, g, 0)),
             pl.BlockSpec((6, 32, CELLS), lambda g: (0, 0, 0)),
-            pl.BlockSpec((32, CELLS), lambda g: (0, 0)),
+            pl.BlockSpec((2, 32, CELLS), lambda g: (0, 0, 0)),
         ],
         out_specs=(big, big),
         compiler_params=pltpu.CompilerParams(vmem_limit_bytes=16 * 2**20),

time: 48.8 us -> 46.4 us (0.951)
  Pallas kernels: 48.1 us -> 45.7 us
    pallas_call x1, Pallas kernels: 44.5 us -> 42.7 us  [body(): pl.pallas_call(exchange_kernel, out_shape=(sds((32, 32, CELLS), bf16), sd...]
    pallas_call x1, Pallas kernels: 3.55 us -> 2.96 us  [body(): pl.pallas_call(correct_kernel, out_shape=(sds((32, 32, CELLS), f32), sds(...]
where the time goes in v5:
time: 46.4 us
  Pallas kernels  45.7 us (98%)
  between operations  0.67 us (1%)
    pallas_call x1, Pallas kernels, body(): pl.pallas_call(exchange_kernel, out_shape=(sds((32, 32, CELLS), bf16), sd...  42.7 us
    pallas_call x1, Pallas kernels, body(): pl.pallas_call(correct_kernel, out_shape=(sds((32, 32, CELLS), f32), sds(...  2.96 us

profile of v5, /device:TPU:1, one launch (start us, length us, event | category | flops | bytes accessed | tf_op | source)
XLA Modules:
  0.0 46.4 jit_solution(13904943066272658804)
XLA Ops:
  0.6 0.0 copy-start
  0.6 0.0 copy-start.1
  0.7 42.7 %shard_map.77 = (bf16[32,32,256]{2,1,0:T(8,128)(2,1)S(1)}, f32[2,32,256]{2,1,0:T(8,128)S(1)}, f32[6,32,256]{2,1,0:T(8,128)S(1)}, f32[2,32,256]{2,1,0:T(8,128)S(1)}) custom-call(f32[32,32,256]{2,1,0:T(8,128)} %it_ref.1, f32[32,32,256]{2,1,0:T(8,128)} %src_ref.1, f32[32,256]{1,0:T(8,128)} %mean_hbm.1, f32[20,32,256]{2,1,0:T(8,128)} %kl_hbm.1, ...), custom_call_target="tpu_custom_call" | custom-call | tf_op jit(solution)/shard_map/pallas_call | solution.py:482
  43.4 0.0 copy-done
  43.4 0.0 copy-done.1
  43.4 3.0 %shard_map.78 = (f32[32,32,256]{2,1,0:T(8,128)}, f32[32,32,256]{2,1,0:T(8,128)}) custom-call(f32[32,32,256]{2,1,0:T(8,128)S(1)} %copy-done, f32[32,32,256]{2,1,0:T(8,128)S(1)} %copy-done.1, bf16[32,32,256]{2,1,0:T(8,128)(2,1)S(1)} %get-tuple-element.6.nat_ref, f32[2,32,256]{2,1,0:T(8,128)S(1)} %get-tuple-element.7.halo_ref, ...), custom_call_target="tpu_custom_call" | custom-call | tf_op jit(solution)/shard_map/pallas_call | solution.py:539
Async XLA Ops:
  0.6 42.7 %copy-start = (f32[32,32,256]{2,1,0:T(8,128)S(1)}, f32[32,32,256]{2,1,0:T(8,128)}, u32[]{:S(2)}) copy-start(f32[32,32,256]{2,1,0:T(8,128)} %it_ref.1) | copy-start | bytes 3145732
  0.6 42.7 %copy-start.1 = (f32[32,32,256]{2,1,0:T(8,128)S(1)}, f32[32,32,256]{2,1,0:T(8,128)}, u32[]{:S(2)}) copy-start(f32[32,32,256]{2,1,0:T(8,128)} %src_ref.1) | copy-start | bytes 3145732

commit v6 on v5

--- a/solution.py
+++ b/solution.py
@@ -114,7 +114,7 @@
 
 def exchange_kernel(
     it_hbm, src_hbm, mean_hbm, kl_hbm, tri_hbm, val_hbm, nat_ref, halo_ref, w_ref, inv_ref,
-    it_ref, src_ref, mean_ref, kl_ref, tri_ref, val_ref, rows_ref, pair_ref, edge_ref, r_ref, mix_ref, table_ref, g_ref, b_ref, nb_ref, s_ref, t_ref, u_ref, v_ref,
+    it_ref, src_ref, mean_ref, kl_ref, tri_ref, val_ref, rows_ref, pair_ref, r_ref, mix_ref, table_ref, g_ref, b_ref, nb_ref, s_ref, t_ref, u_ref, v_ref,
     ce_ref, ch_ref, out_ref, img_ref, fe_ref, fh_ref, c0_ref,
     local_sem, edge_sem, send_sem, recv_sem, coef_sem, back_sem, home_sem, first_sem, pair_sem, go_sem,
 ):
@@ -166,6 +166,13 @@
         for other in (up, down):
             pl.semaphore_signal(barrier, inc=1, device_id=(other, m), device_id_type=MESH)
 
+    for holder, other in ((0, down), (GROUP - 1, up)):
+
+        @pl.when(m == holder)
+        def _():
+            for q in range(1, GROUP, 2):
+                pl.semaphore_signal(barrier, inc=1, device_id=(other, q), device_id_type=MESH)
+
     loads[0].wait()
     swap = swap_matrix(32, 16)
     for g in range(2):
@@ -329,17 +336,18 @@
 
         return rest
 
+    both_modes = pl.ds(pl.multiple_of((m // 2) * 64, 64), 64)
     seven = pl.ds(0, GROUP - 1)
     drain(r_ref.at[1], recv_sem.at[1])
     mix_slot(1)
 
     @pl.when(odd)
     def _():
-        pl.semaphore_wait(barrier, 2)
+        pl.semaphore_wait(barrier, 4)
         for side in range(2):
             drain(pair_ref.at[side, pl.ds(0, 32)], pair_sem.at[2 + side])
-        send(pair_ref.at[1], edge_ref.at[0], (up, m), edge_sem.at[0], edge_sem.at[2])
-        send(pair_ref.at[0], edge_ref.at[1], (down, m), edge_sem.at[1], edge_sem.at[3])
+        send(pair_ref.at[1], r_ref.at[0, both_modes], (up, 0), edge_sem.at[0], recv_sem.at[0])
+        send(pair_ref.at[0], r_ref.at[0, both_modes], (down, GROUP - 1), edge_sem.at[1], recv_sem.at[0])
         send(ce_ref.at[1], ch_ref.at[0], (up, m), coef_sem.at[0], coef_sem.at[2])
         send(ce_ref.at[0], ch_ref.at[1], (down, m), coef_sem.at[1], coef_sem.at[3])
 
@@ -351,21 +359,8 @@
     fill_differences(2)
     finish_row(2)()
 
-    both_modes = pl.ds(pl.multiple_of((m // 2) * 64, 64), 64)
-
     @pl.when(odd)
     def _():
-        for side, holder in ((0, 0), (1, GROUP - 1)):
-            drain(edge_ref.at[side], edge_sem.at[2 + side])
-
-            @pl.when(m == holder)
-            def _():
-                pltpu.make_async_copy(edge_ref.at[side], r_ref.at[0, both_modes], recv_sem.at[0]).start()
-
-            @pl.when(m != holder)
-            def _():
-                send(edge_ref.at[side], r_ref.at[0, both_modes], (d, holder), pair_sem.at[4 + side], recv_sem.at[0])
-
         for side in range(2):
             drain(ch_ref.at[side], coef_sem.at[2 + side])
         send(ch_ref, ch_ref, (d, sibling), coef_sem.at[4], coef_sem.at[5])
@@ -404,10 +399,14 @@
     for side, row in ((0, 0), (1, 31)):
         fe_ref[side] = (src_ref[:, row, :] - img_ref[row].astype(f32)) * first_inv[row : row + 1]
     swap = swap_matrix(16, 32)
-    firsts = [
-        send(fe_ref.at[1], fh_ref.at[0], (up, m), first_sem.at[0], first_sem.at[2]),
-        send(fe_ref.at[0], fh_ref.at[1], (down, m), first_sem.at[1], first_sem.at[3]),
-    ]
+    @pl.when(d < count - 1)
+    def _():
+        send(fe_ref.at[1], fh_ref.at[0], (up, m), first_sem.at[0], first_sem.at[2])
+
+    @pl.when(d > 0)
+    def _():
+        send(fe_ref.at[0], fh_ref.at[1], (down, m), first_sem.at[1], first_sem.at[3])
+
     for k in range(1, 4):
         drain(img_ref.at[seven], home_sem.at[k])
     for g in range(2):
@@ -417,13 +416,9 @@
 
     @pl.when(odd)
     def _():
-        for side, holder in ((0, 0), (1, GROUP - 1)):
-            drain(edge_ref.at[side], edge_sem.at[side])
+        for side in range(2):
+            drain(pair_ref.at[side], edge_sem.at[side])
             drain(ce_ref.at[side], coef_sem.at[side])
-
-            @pl.when(m != holder)
-            def _():
-                drain(edge_ref.at[side], pair_sem.at[4 + side])
 
         drain(ch_ref, coef_sem.at[4])
 
@@ -446,11 +441,17 @@
     forward.wait_send()
     for k in range(4):
         drain(out_ref.at[k, pl.ds(0, 32 * (GROUP - 1))], back_sem.at[k])
-    for copy in firsts:
-        copy.wait_send()
-        copy.wait_recv()
-    halo_ref[0] = fh_ref[0] * first_edge
-    halo_ref[1] = fh_ref[1] * last_edge
+    for side, inside in ((0, d > 0), (1, d < count - 1)):
+
+        @pl.when(inside)
+        def _():
+            drain(fe_ref.at[side], first_sem.at[1 - side])
+            drain(fh_ref.at[side], first_sem.at[2 + side])
+            halo_ref[side] = fh_ref[side]
+
+        @pl.when(jnp.logical_not(inside))
+        def _():
+            halo_ref[side] = jnp.zeros((32, CELLS), f32)
 
 
 STEP = 8
@@ -498,7 +499,6 @@
             pltpu.VMEM((42, 128), f32),
             pltpu.VMEM((32, 32, CELLS), bf16),
             pltpu.VMEM((2, 64, CELLS), bf16),
-            pltpu.VMEM((2, 64, CELLS), bf16),
             pltpu.VMEM((6, P_SIZE, CELLS), bf16),
             pltpu.VMEM((NIB, NF * IB, P_SIZE), bf16),
             pltpu.VMEM((P_SIZE, 64), f32),
@@ -517,14 +517,14 @@
             pltpu.VMEM((2, 32, CELLS), f32),
             pltpu.VMEM((3, 32, CELLS), f32),
             dma((6,)),
-            dma((4,)),
+            dma((2,)),
             dma((6,)),
             dma((6,)),
             dma((6,)),
             dma((4,)),
             dma((4,)),
             dma((4,)),
-            dma((6,)),
+            dma((4,)),
             pltpu.SemaphoreType.REGULAR,
         ],
         compiler_params=pltpu.CompilerParams(

time: 46.4 us -> 43.7 us (0.942)
  Pallas kernels: 45.7 us -> 42.6 us
    pallas_call x1, Pallas kernels: 42.7 us -> 39.7 us  [body(): pl.pallas_call(exchange_kernel, out_shape=(sds((32, 32, CELLS), bf16), sd...]
where the time goes in v6:
time: 43.7 us; the launch traced here: 43.3 us
  Pallas kernels  42.6 us (97%)
  between operations  0.67 us (2%)
    pallas_call x1, Pallas kernels, body(): pl.pallas_call(exchange_kernel, out_shape=(sds((32, 32, CELLS), bf16), sd...  39.7 us
    pallas_call x1, Pallas kernels, body(): pl.pallas_call(correct_kernel, out_shape=(sds((32, 32, CELLS), f32), sds(...  2.96 us

profile of v6, /device:TPU:1, one launch (start us, length us, event | category | flops | bytes accessed | tf_op | source)
XLA Modules:
  0.0 43.3 jit_solution(4541650042941085868)
XLA Ops:
  0.6 0.0 copy-start
  0.6 0.0 copy-start.1
  0.7 39.7 %shard_map.77 = (bf16[32,32,256]{2,1,0:T(8,128)(2,1)S(1)}, f32[2,32,256]{2,1,0:T(8,128)S(1)}, f32[6,32,256]{2,1,0:T(8,128)S(1)}, f32[2,32,256]{2,1,0:T(8,128)S(1)}) custom-call(f32[32,32,256]{2,1,0:T(8,128)} %it_ref.1, f32[32,32,256]{2,1,0:T(8,128)} %src_ref.1, f32[32,256]{1,0:T(8,128)} %mean_hbm.1, f32[20,32,256]{2,1,0:T(8,128)} %kl_hbm.1, ...), custom_call_target="tpu_custom_call" | custom-call | tf_op jit(solution)/shard_map/pallas_call | solution.py:483
  40.3 0.0 copy-done
  40.3 0.0 copy-done.1
  40.4 3.0 %shard_map.78 = (f32[32,32,256]{2,1,0:T(8,128)}, f32[32,32,256]{2,1,0:T(8,128)}) custom-call(f32[32,32,256]{2,1,0:T(8,128)S(1)} %copy-done, f32[32,32,256]{2,1,0:T(8,128)S(1)} %copy-done.1, bf16[32,32,256]{2,1,0:T(8,128)(2,1)S(1)} %get-tuple-element.6.nat_ref, f32[2,32,256]{2,1,0:T(8,128)S(1)} %get-tuple-element.7.halo_ref, ...), custom_call_target="tpu_custom_call" | custom-call | tf_op jit(solution)/shard_map/pallas_call | solution.py:539
Async XLA Ops:
  0.6 39.7 %copy-start = (f32[32,32,256]{2,1,0:T(8,128)S(1)}, f32[32,32,256]{2,1,0:T(8,128)}, u32[]{:S(2)}) copy-start(f32[32,32,256]{2,1,0:T(8,128)} %it_ref.1) | copy-start | bytes 3145732
  0.6 39.7 %copy-start.1 = (f32[32,32,256]{2,1,0:T(8,128)S(1)}, f32[32,32,256]{2,1,0:T(8,128)}, u32[]{:S(2)}) copy-start(f32[32,32,256]{2,1,0:T(8,128)} %src_ref.1) | copy-start | bytes 3145732

commit v7 on v6

--- a/solution.py
+++ b/solution.py
@@ -113,9 +113,9 @@
 
 
 def exchange_kernel(
-    it_hbm, src_hbm, mean_hbm, kl_hbm, tri_hbm, val_hbm, nat_ref, halo_ref, w_ref, inv_ref,
+    it_hbm, src_hbm, mean_hbm, kl_hbm, tri_hbm, val_hbm, upd_ref, res_ref,
     it_ref, src_ref, mean_ref, kl_ref, tri_ref, val_ref, rows_ref, pair_ref, r_ref, mix_ref, table_ref, g_ref, b_ref, nb_ref, s_ref, t_ref, u_ref, v_ref,
-    ce_ref, ch_ref, out_ref, img_ref, fe_ref, fh_ref, c0_ref,
+    ce_ref, ch_ref, out_ref, img_ref, fe_ref, fh_ref, c0_ref, w_ref, inv_ref,
     local_sem, edge_sem, send_sem, recv_sem, coef_sem, back_sem, home_sem, first_sem, pair_sem, go_sem,
 ):
     d = lax.axis_index("dom")
@@ -411,8 +411,22 @@
         drain(img_ref.at[seven], home_sem.at[k])
     for g in range(2):
         block = img_ref[:, 16 * g : 16 * (g + 1), :].reshape(512, CELLS)
-        turned = jnp.dot(swap, block, preferred_element_type=f32).astype(bf16)
-        nat_ref[16 * g : 16 * (g + 1)] = turned.reshape(16, 32, CELLS)
+        turned = jnp.dot(swap, block, preferred_element_type=f32).reshape(16, 32, CELLS)
+        res_ref[16 * g : 16 * (g + 1)] = src_ref[16 * g : 16 * (g + 1)] - turned
+    row = iota((32, CELLS), 0)
+
+    def correct(mode, _):
+        res = res_ref[mode]
+        first = res * inv_ref[0]
+        total = it_ref[mode] + res * inv_ref[1]
+        for f, amount in enumerate((CELLS - NZ, NZ, CELLS - 1, 1)):
+            total = total + w_ref[2 + f] * pltpu.roll(first, amount, 1)
+        above = jnp.where(row == 31, 0.0, pltpu.roll(first, 31, 0))
+        below = jnp.where(row == 0, 0.0, pltpu.roll(first, 1, 0))
+        upd_ref[mode] = total + w_ref[0] * above + w_ref[1] * below
+        return 0
+
+    lax.fori_loop(0, 32, correct, 0, unroll=4)
 
     @pl.when(odd)
     def _():
@@ -447,32 +461,19 @@
         def _():
             drain(fe_ref.at[side], first_sem.at[1 - side])
             drain(fh_ref.at[side], first_sem.at[2 + side])
-            halo_ref[side] = fh_ref[side]
-
-        @pl.when(jnp.logical_not(inside))
-        def _():
-            halo_ref[side] = jnp.zeros((32, CELLS), f32)
-
-
-STEP = 8
-
-
-def correct_kernel(it_ref, src_ref, nat_ref, halo_ref, w_ref, inv_ref, upd_ref, res_ref):
-    row = iota((32, CELLS), 0)
-
-    def update(mode, _):
-        res = src_ref[mode] - nat_ref[mode].astype(f32)
-        res_ref[mode] = res
-        first = res * inv_ref[0]
-        total = it_ref[mode] + res * inv_ref[1]
-        for f, amount in enumerate((CELLS - NZ, NZ, CELLS - 1, 1)):
-            total = total + w_ref[2 + f] * pltpu.roll(first, amount, 1)
-        above = jnp.where(row == 31, halo_ref[1, pl.ds(mode, 1), :], pltpu.roll(first, 31, 0))
-        below = jnp.where(row == 0, halo_ref[0, pl.ds(mode, 1), :], pltpu.roll(first, 1, 0))
-        upd_ref[mode] = total + w_ref[0] * above + w_ref[1] * below
-        return 0
-
-    lax.fori_loop(0, STEP, update, 0, unroll=4)
+            edge = 31 * side
+            weight = w_ref[1 - side, edge : edge + 1]
+            upd_ref[:, edge, :] = upd_ref[:, edge, :] + weight * fh_ref[side]
+
+
+def store_kernel(upd_ref, res_ref, upd_hbm, res_hbm, sem):
+    copies = [
+        pltpu.make_async_copy(a, b, sem.at[i]) for i, (a, b) in enumerate(((upd_ref, upd_hbm), (res_ref, res_hbm)))
+    ]
+    for copy in copies:
+        copy.start()
+    for copy in copies:
+        copy.wait()
 
 
 def body(iterate, source, mean_coef, kl_fields, tri_index, tri_value):
@@ -480,16 +481,12 @@
     vm = pl.BlockSpec(memory_space=pltpu.VMEM)
     hbm = pl.BlockSpec(memory_space=pltpu.HBM)
     dma = pltpu.SemaphoreType.DMA
-    natural, halo, w, inv = pl.pallas_call(
+    block = sds((32, 32, CELLS), f32)
+    updated, residual = pl.pallas_call(
         exchange_kernel,
-        out_shape=(
-            sds((32, 32, CELLS), bf16),
-            sds((2, 32, CELLS), f32),
-            sds((6, 32, CELLS), f32),
-            sds((2, 32, CELLS), f32),
-        ),
+        out_shape=(block, block),
         in_specs=[hbm] * 6,
-        out_specs=(vm, vm, vm, vm),
+        out_specs=(vm, vm),
         scratch_shapes=[
             pltpu.VMEM((32, 32, CELLS), f32),
             pltpu.VMEM((32, 32, CELLS), f32),
@@ -516,6 +513,8 @@
             pltpu.VMEM((2, 32, CELLS), f32),
             pltpu.VMEM((2, 32, CELLS), f32),
             pltpu.VMEM((3, 32, CELLS), f32),
+            pltpu.VMEM((6, 32, CELLS), f32),
+            pltpu.VMEM((2, 32, CELLS), f32),
             dma((6,)),
             dma((2,)),
             dma((6,)),
@@ -535,22 +534,14 @@
         for x in (iterate, source, mean_coef, kl_fields, tri_index.T, tri_value.reshape(42, 128))
     ])
 
-    big = pl.BlockSpec((STEP, 32, CELLS), lambda g: (g, 0, 0))
     return pl.pallas_call(
-        correct_kernel,
-        out_shape=(sds((32, 32, CELLS), f32), sds((32, 32, CELLS), f32)),
-        grid=(32 // STEP,),
-        in_specs=[
-            big,
-            big,
-            big,
-            pl.BlockSpec((2, STEP, CELLS), lambda g: (0, g, 0)),
-            pl.BlockSpec((6, 32, CELLS), lambda g: (0, 0, 0)),
-            pl.BlockSpec((2, 32, CELLS), lambda g: (0, 0, 0)),
-        ],
-        out_specs=(big, big),
-        compiler_params=pltpu.CompilerParams(vmem_limit_bytes=16 * 2**20),
-    )(iterate, source, natural, halo, w, inv)
+        store_kernel,
+        out_shape=(block, block),
+        in_specs=[vm, vm],
+        out_specs=(pl.BlockSpec(memory_space=pl.ANY),) * 2,
+        scratch_shapes=[dma((2,))],
+        compiler_params=pltpu.CompilerParams(vmem_limit_bytes=8 * 2**20),
+    )(updated, residual)
 
 
 def solution(mesh):

time: 43.7 us -> 42.9 us (0.982)
  Pallas kernels: 42.6 us -> 42.1 us
    pallas_call x2, Pallas kernels: 42.6 us -> 42.1 us  [the longest x1 40.8 us: body(): pl.pallas_call(exchange_kernel, out_shape=(block, block), in_specs=[hbm]...]
where the time goes in v7:
time: 42.9 us; the launch traced here: 42.8 us
  Pallas kernels  42.1 us (98%)
  between operations  0.64 us (1%)
    pallas_call x1, Pallas kernels, body(): pl.pallas_call(exchange_kernel, out_shape=(block, block), in_specs=[hbm]...  40.8 us
    pallas_call x1, Pallas kernels, body(): pl.pallas_call(store_kernel, out_shape=(block, block), in_specs=[vm, vm],...  1.33 us

profile of v7, /device:TPU:1, one launch (start us, length us, event | category | flops | bytes accessed | tf_op | source)
XLA Modules:
  0.0 42.8 jit_solution(4786135649856912394)
XLA Ops:
  0.6 40.8 %shard_map.77 = (f32[32,32,256]{2,1,0:T(8,128)S(1)}, f32[32,32,256]{2,1,0:T(8,128)S(1)}) custom-call(f32[32,32,256]{2,1,0:T(8,128)} %it_hbm.1, f32[32,32,256]{2,1,0:T(8,128)} %src_hbm.1, f32[32,256]{1,0:T(8,128)} %mean_hbm.1, f32[20,32,256]{2,1,0:T(8,128)} %kl_hbm.1, s32[3,5376]{1,0:T(4,128)} %bitcast.2, f32[42,128]{1,0:T(8,128)} %bitcast.3), custom_call_target="tpu_custom_call" | custom-call | tf_op jit(solution)/shard_map/pallas_call | solution.py:485
  41.4 1.3 %shard_map.78 = (f32[32,32,256]{2,1,0:T(8,128)}, f32[32,32,256]{2,1,0:T(8,128)}) custom-call(f32[32,32,256]{2,1,0:T(8,128)S(1)} %get-tuple-element.4.upd_ref, f32[32,32,256]{2,1,0:T(8,128)S(1)} %get-tuple-element.5.res_ref), custom_call_target="tpu_custom_call" | custom-call | tf_op jit(solution)/shard_map/pallas_call | solution.py:537
